TPU v7x, 512 devices: a whole 4x8x8 slice. The times are simulated.
512 devices in a mesh: dp: 32 (over z, x), tensor: 16 (over y, core).
Axes of the slice: x: 4, y: 8, z: 8, core: 2. Of those that a mesh axis runs over, the one named last changes fastest.
Arguments:
- tokens: int32 [64, 4], P('dp'), may hold values from 0 to 77823
- embed_table: bfloat16 [77824, 3584], P('dp', 'tensor'), may hold values from -6 to 6
- norm_gain: bfloat16 [3584], P('tensor'), may hold values from 0.099609375 to 1.8984375
- w_query: bfloat16 [3584, 2048], P('tensor'), may hold values from -0.09375 to 0.09375
- w_key_value: bfloat16 [3584, 1024], P('tensor'), may hold values from -0.09375 to 0.09375
- cache_keys: bfloat16 [64, 4, 64, 128], P('dp'), may hold values from -6 to 6
- cache_values: bfloat16 [64, 4, 64, 128], P('dp'), may hold values from -6 to 6
- cache_len: int32 [64], P('dp'), may hold values from 1 to 64, 2048 in all
- teacher_rows: bfloat16 [512, 8192], P('dp', 'tensor'), may hold values from -6 to 6
- w_llama: bfloat16 [8192, 2, 14336], P('tensor', None, 'dp'), may hold values from -0.0625 to 0.0625
- w_qwen: bfloat16 [8192, 2, 14784], P('tensor', None, 'dp'), may hold values from -0.0625 to 0.0625
- rollout_len: int32 [32, 4], P('dp'), may hold values from 1 to 8, 16 in all within a row
- teacher_of: int32 [32, 4], P('dp'), may hold values from 0 to 1
Outputs:
- attn_out: bfloat16 [64, 4, 2048], P('dp', None, 'tensor')
- llama_hidden: bfloat16 [512, 14336], P('tensor', 'dp')
- qwen_hidden: bfloat16 [512, 14784], P('tensor', 'dp')
Inputs may be any that keep to these rules, and one draw needn't show every extreme that they name: `cache_len`: at least one rollout fills all 64 slots. `rollout_len`: each row sums to 16; the longest rollout of a row has 8 token rows.
All inputs are finite; a program needn't handle non-finite values. No bound on the sum of `cache_len` on one device may be relied on, other than what follows from the above.
Results may differ from a plain program's by a relative error of at most 0.01.
Values may be sent and summed in bfloat16 or wider, within the bound.
No kernel may reach another device: no remote copies, remote signals or barrier semaphores. Data moves between devices by JAX's collectives and lax.ppermute only.
A program may use at most 64 MiB of HBM per device.

v0:
```python
import math

import jax
import jax.numpy as jnp
from jax import lax
from jax.sharding import PartitionSpec as P

DS = 3584
HEADS = 16
KVH = 4
HD = 128
TT_DEV = 16


def row_owner(rollout_len, teacher_of, per_group):
    ends = jnp.cumsum(rollout_len, axis=1)
    offset = jnp.arange(per_group, dtype=jnp.int32)
    which = jnp.sum((offset[None, :, None] >= ends[:, None, :]).astype(jnp.int32), axis=2)
    slots = jnp.arange(rollout_len.shape[1], dtype=jnp.int32)
    pick = (which[:, :, None] == slots[None, None, :]).astype(jnp.int32)
    return jnp.sum(pick * teacher_of[:, None, :], axis=2).reshape(-1)


def attend(query, keys_cache, values_cache, keys_new, values_new, cache_len):
    scale = 1.0 / math.sqrt(query.shape[-1])
    query_f = query.astype(jnp.float32)
    score_cache = jnp.einsum("bshd,bhld->bshl", query_f, keys_cache.astype(jnp.float32)) * scale
    score_new = jnp.einsum("bshd,bthd->bsht", query_f, keys_new.astype(jnp.float32)) * scale
    live = jnp.arange(keys_cache.shape[2], dtype=jnp.int32)[None, :] < cache_len[:, None]
    steps = query.shape[1]
    causal = jnp.arange(steps)[:, None] >= jnp.arange(steps)[None, :]
    score_cache = jnp.where(live[:, None, None, :], score_cache, -jnp.inf)
    score_new = jnp.where(causal[None, :, None, :], score_new, -jnp.inf)
    top = jnp.maximum(jnp.max(score_cache, axis=3), jnp.max(score_new, axis=3))[..., None]
    exp_cache = jnp.exp(score_cache - top)
    exp_new = jnp.exp(score_new - top)
    total = jnp.sum(exp_cache, axis=3, keepdims=True) + jnp.sum(exp_new, axis=3, keepdims=True)
    prob_cache = (exp_cache / total).astype(jnp.bfloat16)
    prob_new = (exp_new / total).astype(jnp.bfloat16)
    mixed = jnp.einsum(
        "bshl,bhld->bshd", prob_cache.astype(jnp.float32), values_cache.astype(jnp.float32)
    )
    mixed = mixed + jnp.einsum(
        "bsht,bthd->bshd", prob_new.astype(jnp.float32), values_new.astype(jnp.float32)
    )
    return mixed.astype(jnp.bfloat16)


def shards(
    tokens,
    embed_table,
    norm_gain,
    w_query,
    w_key_value,
    cache_keys,
    cache_values,
    cache_len,
    teacher_rows,
    w_llama,
    w_qwen,
    rollout_len,
    teacher_of,
):
    all_tokens, all_lengths, all_owners = (
        lax.all_gather(tokens, "dp", axis=0, tiled=True),
        lax.all_gather(rollout_len, "dp", axis=0, tiled=True),
        lax.all_gather(teacher_of, "dp", axis=0, tiled=True),
    )
    table_rows = embed_table.shape[0]
    local_id = all_tokens - lax.axis_index("dp") * table_rows
    inside = jnp.logical_and(local_id >= 0, local_id < table_rows)
    picked = jnp.take(embed_table, jnp.clip(local_id, 0, table_rows - 1), axis=0)
    term = jnp.where(inside[:, :, None], picked.astype(jnp.float32), 0.0)
    embedded = lax.psum_scatter(term, "dp", scatter_dimension=0, tiled=True).astype(jnp.bfloat16)
    rollouts, steps, columns = embedded.shape
    x_float = embedded.astype(jnp.float32)
    scaled = (x_float * norm_gain.astype(jnp.float32)).astype(jnp.bfloat16).reshape(-1, columns)
    query_part = jnp.dot(scaled, w_query, preferred_element_type=jnp.float32)
    pair_part = jnp.dot(scaled, w_key_value, preferred_element_type=jnp.float32)
    squares = jnp.sum(x_float * x_float, axis=2).reshape(-1)
    heads_here = HEADS // lax.axis_size("tensor")
    head_first = lax.axis_index("tensor") * heads_here
    query_sum, pair_sum, square_sum = lax.psum((query_part, pair_part, squares), "tensor")
    query_own = lax.dynamic_slice_in_dim(query_sum, head_first * HD, heads_here * HD, 1)
    inverse = lax.rsqrt(square_sum / DS + 1e-06)[:, None]
    query = (query_own * inverse).astype(jnp.bfloat16).reshape(rollouts, steps, heads_here, HD)
    key_value = (pair_sum * inverse).astype(jnp.bfloat16).reshape(rollouts, steps, 2, KVH, HD)
    kv_index = (head_first + jnp.arange(heads_here, dtype=jnp.int32)) // (HEADS // KVH)
    keys_cache = jnp.take(cache_keys, kv_index, axis=1)
    values_cache = jnp.take(cache_values, kv_index, axis=1)
    keys_new = jnp.take(key_value[:, :, 0], kv_index, axis=2)
    values_new = jnp.take(key_value[:, :, 1], kv_index, axis=2)
    attn_out = attend(query, keys_cache, values_cache, keys_new, values_new, cache_len).reshape(
        rollouts, steps, heads_here * HD
    )
    llama_cols = w_llama.shape[2]
    qwen_cols = w_qwen.shape[2]
    llama_flat = w_llama.reshape(w_llama.shape[0], 2 * llama_cols)
    qwen_flat = w_qwen.reshape(w_qwen.shape[0], 2 * qwen_cols)
    piece = lax.all_gather(teacher_rows, "dp", axis=0, tiled=True)
    first_part = jnp.dot(piece, llama_flat, preferred_element_type=jnp.float32)
    second_part = jnp.dot(piece, qwen_flat, preferred_element_type=jnp.float32)
    partial_rows = jnp.concatenate([first_part, second_part], axis=1)
    rows_here = partial_rows.shape[0] // lax.axis_size("tensor")
    row_first = lax.axis_index("tensor") * rows_here
    summed_all = lax.psum(partial_rows, "tensor")
    summed = lax.dynamic_slice_in_dim(summed_all, row_first, rows_here, 0)
    owner_all = row_owner(all_lengths, all_owners, TT_DEV)
    owner = lax.dynamic_slice_in_dim(owner_all, row_first, rows_here, 0)
    gate_llama = summed[:, :llama_cols]
    up_llama = summed[:, llama_cols : 2 * llama_cols]
    gate_qwen = summed[:, 2 * llama_cols : 2 * llama_cols + qwen_cols]
    up_qwen = summed[:, 2 * llama_cols + qwen_cols :]
    llama_hidden = jnp.where((owner == 0)[:, None], jax.nn.silu(gate_llama) * up_llama, 0.0).astype(
        jnp.bfloat16
    )
    qwen_hidden = jnp.where((owner == 1)[:, None], jax.nn.silu(gate_qwen) * up_qwen, 0.0).astype(
        jnp.bfloat16
    )
    return (attn_out, llama_hidden, qwen_hidden)


def solution(mesh):
    return jax.shard_map(
        shards,
        mesh=mesh,
        in_specs=(
            P("dp", None),
            P("dp", "tensor"),
            P("tensor"),
            P("tensor", None),
            P("tensor", None),
            P("dp", None, None, None),
            P("dp", None, None, None),
            P("dp"),
            P("dp", "tensor"),
            P("tensor", None, "dp"),
            P("tensor", None, "dp"),
            P("dp", None),
            P("dp", None),
        ),
        out_specs=(P("dp", None, "tensor"), P("tensor", "dp"), P("tensor", "dp")),
        check_vma=False,
    )
```

profile of v0, /device:TPU:1, one launch (start us, length us, event | category | flops | bytes accessed | tf_op | source)
XLA Modules:
  0.0 396.1 jit_solution(5077311815255898789)
XLA Ops:
  7.2 0.0 copy-start
  7.2 0.0 all-reduce.6.cloned.1.call-start
  7.2 40.1 %all-gather = s32[32,2,4]{2,1,0:T(2,128)S(1)} all-gather(s32[1,2,4]{2,1,0:T(2,128)} %bitcast.99), channel_id=1, replica_groups=mesh['dp'=32,'tensor'=16] {'dp'}, dimensions={0}, use_global_device_ids=true | all-gather | bytes 1056 | tf_op jit(solution)/shard_map/all_gather | solution.py:65
  47.3 0.1 copy.94
  47.4 0.1 copy.97
  47.6 0.0 copy-start.3
  47.6 1.9 copy.98
  49.5 0.1 reshape.298
  49.6 1.2 gather_fusion
  50.8 0.1 copy.110
  51.0 0.2 convert_select_fusion
  51.2 114.2 %all-reduce.7 = bf16[64,4,224]{2,1,0:T(4,128)(2,1)S(1)} all-reduce(f32[64,4,224]{2,1,0:T(4,128)S(1)} %convert_select_fusion), channel_id=2, replica_groups=mesh['dp'=32,'tensor'=16] {'dp'}, use_global_device_ids=true, to_apply=%region_0.2.clone | all-reduce | flops 57344 | bytes 344064
  165.4 1.3 dynamic-slice.14
  167.3 0.1 fusion.23
  167.4 35.3 %all_gather.15 = bf16[512,512]{1,0:T(8,128)(2,1)S(1)} all-gather(bf16[16,512]{1,0:T(8,128)(2,1)S(1)} %copy-done.3), channel_id=1, replica_groups=mesh['dp'=32,'tensor'=16] {'dp'}, dimensions={0}, use_global_device_ids=true | all-gather | bytes 540672 | tf_op jit(solution)/shard_map/all_gather | solution.py:100
  202.7 1.3 copy.105
  204.1 0.2 reshape.181
  204.3 0.7 fusion.53
  205.0 0.0 copy-start.1
  205.0 0.7 fusion.52
  205.6 0.5 copy-done.1
  206.1 0.8 fusion.50
  207.0 2.2 pad_maximum_fusion
  209.2 0.0 all-reduce.6.cloned.1.call-update
  209.3 1.0 copy-done.2
  210.2 0.2 fusion.51
  210.4 0.1 reshape.171
  210.5 92.0 %all-reduce.1 = (f32[8]{0:T(128)S(1)}, f32[8,1024]{1,0:T(8,128)S(1)}) all-reduce(f32[8]{0:T(128)S(1)} %reshape.171, f32[8,1024]{1,0:T(8,128)S(1)} %fusion.51), channel_id=1, replica_groups=mesh['dp'=32,'tensor'=16] {'tensor'}, use_global_device_ids=true, to_apply=%region_3.5 | all-reduce | flops 8200 | bytes 65600 | tf_op jit(solution)/shard_map/psum | solution.py:83
  302.5 31.4 %all-gather.2 = s32[32,1,4]{2,1,0:T(1,128)S(1)} all-gather(s32[1,1,4]{2,1,0:T(1,128)S(1)} %bitcast.100), channel_id=1, replica_groups=mesh['dp'=32,'tensor'=16] {'dp'}, dimensions={0}, use_global_device_ids=true | all-gather | bytes 528 | tf_op jit(solution)/shard_map/all_gather | solution.py:67
  333.9 0.1 copy.103
  334.0 30.2 %all-gather.1 = s32[32,1,4]{2,1,0:T(1,128)S(1)} all-gather(s32[1,1,4]{2,1,0:T(1,128)S(1)} %bitcast.101), channel_id=1, replica_groups=mesh['dp'=32,'tensor'=16] {'dp'}, dimensions={0}, use_global_device_ids=true | all-gather | bytes 528 | tf_op jit(solution)/shard_map/all_gather | solution.py:66
  364.2 0.1 copy.102
  364.4 0.1 copy.104
  364.5 0.1 reshape.179
  364.6 0.1 broadcast_compare_fusion
  364.6 0.1 iota_compare_fusion.3
  364.7 0.1 multiply_convert_fusion
  364.8 16.7 %all-reduce.6.cloned.1.call-done = (f32[8,2048]{1,0:T(8,128)}, f32[512,1820]{0,1:T(8,128)}) async-done(((f32[8,2048]{1,0:T(8,128)}, f32[512,1820]{0,1:T(8,128)}), (f32[8,2048]{1,0:T(8,128)}, f32[512,1820]{0,1:T(8,128)})) %all-reduce.6.cloned.1.call-update) | async-done | bytes 3792912 | tf_op jit(solution)/shard_map/psum | solution.py:83
  381.5 0.8 multiply_convert_fusion.1
  382.3 1.0 fusion.48
  383.2 0.1 fusion.49
  383.4 0.2 fusion.24
  383.6 1.2 fusion.10
  384.8 0.7 copy.107
  385.5 1.3 fusion.8
  386.8 0.7 copy.108
  387.5 0.9 fusion.14
  388.5 0.8 fusion.5
  (29 shorter events, 0.3 us)
Async XLA Ops:
  7.2 197.8 %copy-start = (bf16[512,2,448]{0,2,1:T(8,128)(2,1)S(1)}, bf16[512,2,448]{0,2,1:T(8,128)(2,1)}, u32[]{:S(2)}) copy-start(bf16[512,2,448]{0,2,1:T(8,128)(2,1)} %param.26) | copy-start | bytes 2752516
  7.2 374.3 %all-reduce.6.cloned.1.call-start = ((), (), s32[]{:S(2)}) async-start(), calls=%async_computation | async-start | bytes 7602176 | tf_op jit(solution)/shard_map/psum | solution.py:83
  47.6 117.8 %copy-start.6 = (bf16[224]{0:T(256)(128)(2,1)S(1)}, bf16[224]{0:T(256)(128)(2,1)}, u32[]{:S(2)}) copy-start(bf16[224]{0:T(256)(128)(2,1)} %param.19) | copy-start | bytes 1348
  47.6 119.8 %copy-start.3 = (bf16[16,512]{1,0:T(8,128)(2,1)S(1)}, bf16[16,512]{1,0:T(8,128)(2,1)}, u32[]{:S(2)}) copy-start(bf16[16,512]{1,0:T(8,128)(2,1)} %param.25) | copy-start | bytes 49156
  205.0 1.2 copy-start.1
  209.2 1.0 copy-start.2
  209.2 93.3 %copy-start.4 = (s32[1,4]{1,0:T(1,128)S(1)}, s32[1,4]{1,0:T(1,128)}, u32[]{:S(2)}) copy-start(s32[1,4]{1,0:T(1,128)} %param.29) | copy-start | bytes 52
  209.2 124.8 %copy-start.5 = (s32[1,4]{1,0:T(1,128)S(1)}, s32[1,4]{1,0:T(1,128)}, u32[]{:S(2)}) copy-start(s32[1,4]{1,0:T(1,128)} %param.28) | copy-start | bytes 52
  209.2 155.4 %copy-start.7 = (s32[2]{0:T(128)S(1)}, s32[2]{0:T(128)}, u32[]{:S(2)}) copy-start(s32[2]{0:T(128)} %param.24) | copy-start | bytes 28
Sparse Core Ops, SparseCore 0:
  209.4 172.0 all-reduce.5
where the time goes:
time: 397 us; the launch traced here: 396 us
  blocking collectives  343 us (86%)
  waiting for transfers between devices  16.7 us (4%)
  between operations  14.9 us (4%)
  local copies, waits for them, and re-layouts  9.69 us (2%)
  other arithmetic  6.34 us (2%)
  matrix products  5.2 us (1%)
    unnamed x1, blocking collectives  114 us
    psum x1, blocking collectives, shards(): lax.psum((query_part, pair_part, squares), 'tensor')  92 us
    all_gather x1, blocking collectives, shards(): lax.all_gather(tokens, 'dp', axis=0, tiled=True)  40.1 us
    all_gather x1, blocking collectives, shards(): piece = lax.all_gather(teacher_rows, 'dp', axis=0, tiled=True)  35.3 us
    all_gather x1, blocking collectives, shards(): lax.all_gather(teacher_of, 'dp', axis=0, tiled=True)  31.4 us
    all_gather x1, blocking collectives, shards(): lax.all_gather(rollout_len, 'dp', axis=0, tiled=True)  30.2 us
    psum x1, waiting for transfers between devices, shards(): lax.psum((query_part, pair_part, squares), 'tensor')  16.7 us
  transfers between devices with their start and end apart: 1, of which 1 were waited for; matrix products, arithmetic and copies ran while one was open for 0% of the time, Pallas kernels for 0%

commit v1 on v0

v1 whole, which is shorter than its diff:
```python
import functools
import math

import jax
import jax.numpy as jnp
from jax import lax
from jax.experimental import pallas as pl
from jax.experimental.pallas import tpu as pltpu
from jax.sharding import PartitionSpec as P

DS = 3584
HD = 128
KVH = 4
EPS = 1e-06
VMEM = pltpu.MemorySpace.VMEM
SMEM = pltpu.MemorySpace.SMEM
F32 = jnp.float32
BF16 = jnp.bfloat16


def nt_dot(a, b):
    return lax.dot_general(a, b, (((1,), (1,)), ((), ())), preferred_element_type=F32)


def fetch_kernel(first_ref, ints_ref, table_ref, rows_ref, out_ref):
    groups, _, _ = ints_ref.shape
    per = out_ref.shape[1] // 2
    columns, vocab = table_ref.shape
    width = rows_ref.shape[1]
    ids = jnp.broadcast_to(ints_ref[...].astype(F32), (groups, per, ints_ref.shape[2]))
    lane = lax.broadcasted_iota(jnp.int32, ids.shape, 2)
    sub = lax.broadcasted_iota(jnp.int32, ids.shape, 1)
    ids = jnp.sum(jnp.where(lane == sub, ids, 0.0), axis=2, keepdims=True)
    ids = ids.astype(jnp.int32).reshape(groups * per, 1) - first_ref[0]
    place = lax.broadcasted_iota(jnp.int32, (groups * per, vocab), 1)
    hot = jnp.where(ids == place, 1.0, 0.0).astype(BF16)
    found = nt_dot(hot, table_ref[...]).astype(BF16).reshape(groups, per, columns)
    out_ref[:, :, :width] = jnp.broadcast_to(rows_ref[...][None], (groups,) + rows_ref.shape)
    out_ref[:, 0:per, width : width + HD] = found[:, :, :HD]
    rest = jnp.concatenate(
        [found[:, :, HD:], jnp.zeros((groups, per, 2 * HD - columns), BF16)], axis=2
    )
    out_ref[:, per:, width : width + HD] = rest


def part_kernel(
    side_ref, rows_ref, found_ref, ints_ref, gain_ref, wq_ref, wkv_ref, wl_ref, ww_ref,
    out_ref, query_ref,
):
    places, _, count, width = rows_ref.shape
    side = side_ref[0]
    per = count // 4
    columns = wq_ref.shape[0]
    half = wl_ref.shape[1]
    wide = ww_ref.shape[1]
    half_pad = (out_ref.shape[2] - HD) // 2

    rows = rows_ref[...].reshape(places * count, width)
    ints = ints_ref[...].reshape(places * 2, 1, ints_ref.shape[-1])
    lens = [ints[:, :, per + k : per + k + 1] for k in range(4)]
    kinds = [ints[:, :, per + 4 + k : per + 5 + k] for k in range(4)]
    offset = lax.broadcasted_iota(jnp.int32, (places * 2, count // 2, 1), 1)
    ends = [lens[0], lens[0] + lens[1], lens[0] + lens[1] + lens[2]]
    owner = jnp.where(
        offset < ends[0],
        kinds[0],
        jnp.where(offset < ends[1], kinds[1], jnp.where(offset < ends[2], kinds[2], kinds[3])),
    )
    first = owner.reshape(places * count, 1) == 0
    for k in range(2):
        one = nt_dot(rows, wl_ref[k])
        two = nt_dot(rows, ww_ref[k])
        one = jnp.concatenate([one, jnp.zeros((places * count, half_pad - half), F32)], axis=1)
        two = jnp.concatenate([two, jnp.zeros((places * count, half_pad - wide), F32)], axis=1)
        both = jnp.where(first, one, two).astype(BF16)
        out_ref[:, :, k * half_pad : (k + 1) * half_pad] = both.reshape(places, count, half_pad)

    embedded = jnp.sum(found_ref[...].astype(F32), axis=0)
    x = jnp.concatenate([embedded[:per], embedded[per:]], axis=1)[:, :columns]
    scaled = (x * gain_ref[...].astype(F32)).astype(BF16)
    query_ref[...] = jnp.dot(scaled, wq_ref[...], preferred_element_type=F32)
    pair = jnp.dot(scaled, wkv_ref[...], preferred_element_type=F32)
    squares = jnp.broadcast_to(jnp.sum(x * x, axis=1, keepdims=True), (per, HD))
    base = 2 * half_pad
    for p in range(places):
        start = pl.multiple_of((2 * p + side) * HD, HD)
        head = (2 * p * KVH) // (2 * places)
        key = pair[:, head * HD : (head + 1) * HD]
        value = pair[:, (KVH + head) * HD : (KVH + head + 1) * HD]
        own = query_ref[:, pl.ds(start, HD)]
        out_ref[p, :, base : base + HD] = jnp.concatenate([own, key, value, squares], axis=0).astype(BF16)


def last_kernel(
    sizes_ref, parts_ref, ints_ref, keys_ref, values_ref, attn_ref, llama_ref, qwen_ref
):
    count = parts_ref.shape[1]
    per = count // 4
    half_pad = (parts_ref.shape[2] - HD) // 2
    half = llama_ref.shape[1]
    wide = qwen_ref.shape[1]
    total = jnp.sum(parts_ref[...].astype(F32), axis=0)
    gate = total[:, :half_pad]
    up = total[:, half_pad : 2 * half_pad]
    hidden = gate / (1.0 + jnp.exp(-gate)) * up
    ints = ints_ref[...]
    lens = [ints[:, :, per + k : per + k + 1] for k in range(4)]
    kinds = [ints[:, :, per + 4 + k : per + 5 + k] for k in range(4)]
    offset = lax.broadcasted_iota(jnp.int32, (2, count // 2, 1), 1)
    ends = [lens[0], lens[0] + lens[1], lens[0] + lens[1] + lens[2]]
    owner = jnp.where(
        offset < ends[0],
        kinds[0],
        jnp.where(offset < ends[1], kinds[1], jnp.where(offset < ends[2], kinds[2], kinds[3])),
    )
    first = owner.reshape(count, 1) == 0
    llama_ref[...] = jnp.where(first, hidden, 0.0)[:, :half].astype(BF16)
    qwen_ref[...] = jnp.where(first, 0.0, hidden)[:, :wide].astype(BF16)

    student = total[:, 2 * half_pad :]
    inverse = lax.rsqrt(student[3 * per :] / DS + EPS)
    query = (student[:per] * inverse).astype(BF16)
    key = (student[per : 2 * per] * inverse).astype(BF16)
    value = (student[2 * per : 3 * per] * inverse).astype(BF16)
    rollouts, _, slots, _ = keys_ref.shape
    steps = per // rollouts
    scale = 1.0 / math.sqrt(HD)
    score_new = nt_dot(query, key) * scale
    row = lax.broadcasted_iota(jnp.int32, (per, per), 0)
    col = lax.broadcasted_iota(jnp.int32, (per, per), 1)
    fits = jnp.logical_and(row // steps == col // steps, col <= row)
    score_new = jnp.where(fits, score_new, -jnp.inf)
    for b in range(rollouts):
        score = nt_dot(query, keys_ref[b, 0]) * scale
        slot = lax.broadcasted_iota(jnp.int32, (per, slots), 1)
        score = jnp.where(slot < sizes_ref[b], score, -jnp.inf)
        mine = score_new[b * steps : (b + 1) * steps]
        score = score[b * steps : (b + 1) * steps]
        top = jnp.maximum(
            jnp.max(score, axis=1, keepdims=True), jnp.max(mine, axis=1, keepdims=True)
        )
        old_exp = jnp.exp(score - top)
        new_exp = jnp.exp(mine - top)
        whole = jnp.sum(old_exp, axis=1, keepdims=True) + jnp.sum(new_exp, axis=1, keepdims=True)
        old = (old_exp / whole).astype(BF16)
        new = (new_exp / whole).astype(BF16)
        mixed = jnp.dot(old, values_ref[b, 0], preferred_element_type=F32)
        mixed = mixed + jnp.dot(new, value, preferred_element_type=F32)
        attn_ref[b] = mixed.astype(BF16)


def whole_spec(array):
    rank = len(array.shape)
    return pl.BlockSpec(array.shape, lambda *_: (0,) * rank)


def shards(
    tokens,
    embed_table,
    norm_gain,
    w_query,
    w_key_value,
    cache_keys,
    cache_values,
    cache_len,
    teacher_rows,
    w_llama,
    w_qwen,
    rollout_len,
    teacher_of,
):
    groups = lax.axis_size("dp")
    targets = lax.axis_size("tensor")
    places = targets // 2
    dp_index = lax.axis_index("dp")
    tensor_index = lax.axis_index("tensor")
    core = tensor_index % 2
    rollouts, steps = tokens.shape
    per = rollouts * steps
    vocab, columns = embed_table.shape
    count, width = teacher_rows.shape
    rows_here = groups * count // targets

    ints = jnp.concatenate([tokens.reshape(1, per), rollout_len, teacher_of], axis=1)
    ints = jnp.broadcast_to(ints[None], (groups, 1, ints.shape[1]))
    ints = lax.all_to_all(ints, "dp", 0, 0, tiled=True)

    table = embed_table.T
    sent = pl.pallas_call(
        fetch_kernel,
        grid_spec=pltpu.PrefetchScalarGridSpec(
            num_scalar_prefetch=1,
            grid=(1,),
            in_specs=[whole_spec(ints), whole_spec(table), whole_spec(teacher_rows)],
            out_specs=pl.BlockSpec((groups, count, width + HD), lambda *_: (0, 0, 0)),
        ),
        out_shape=jax.ShapeDtypeStruct((groups, count, width + HD), BF16),
        name="fetch",
    )((dp_index * vocab).reshape(1), ints, table, teacher_rows)
    held = lax.all_to_all(sent, "dp", 0, 0, tiled=True)

    by_place = held.reshape(places, 2, rows_here, width + HD)
    ints_place = ints.reshape(places, 2, 2, 1, ints.shape[2])
    first_w = jnp.transpose(w_llama, (1, 2, 0))
    second_w = jnp.transpose(w_qwen, (1, 2, 0))
    gain = norm_gain.reshape(1, columns)
    half_pad = 512
    total_width = 2 * half_pad + HD

    def part(side):
        return pl.pallas_call(
            part_kernel,
            grid_spec=pltpu.PrefetchScalarGridSpec(
                num_scalar_prefetch=1,
                grid=(1,),
                in_specs=[
                    pl.BlockSpec((places, 1, rows_here, width), lambda i, s: (0, s[0], 0, 0)),
                    pl.BlockSpec((groups, count, HD), lambda i, s: (0, 0, width // HD)),
                    pl.BlockSpec(
                        (places, 1, 2, 1, ints.shape[2]), lambda i, s: (0, s[0], 0, 0, 0)
                    ),
                    whole_spec(gain),
                    whole_spec(w_query),
                    whole_spec(w_key_value),
                    whole_spec(first_w),
                    whole_spec(second_w),
                ],
                out_specs=pl.BlockSpec((places, rows_here, total_width), lambda *_: (0, 0, 0)),
                scratch_shapes=[pltpu.VMEM((per, w_query.shape[1]), F32)],
            ),
            out_shape=jax.ShapeDtypeStruct((places, rows_here, total_width), BF16),
            name="part",
        )(side.reshape(1), by_place, held, ints_place, gain, w_query, w_key_value, first_w, second_w)

    theirs = part(1 - core)
    theirs = lax.ppermute(theirs, "tensor", [(i, i ^ 1) for i in range(targets)])
    ours = part(core)
    joined = (theirs.astype(F32) + ours.astype(F32)).astype(BF16)
    lines = [[2 * p + c for p in range(places)] for c in range(2)]
    parts = lax.all_to_all(joined, "tensor", 0, 0, axis_index_groups=lines, tiled=True)

    kv = (tensor_index * KVH) // targets
    slots = cache_keys.shape[2]
    scalars = jnp.concatenate(
        [cache_len, jnp.stack([tensor_index, kv]).astype(jnp.int32)]
    )
    attn, llama, qwen = pl.pallas_call(
        last_kernel,
        grid_spec=pltpu.PrefetchScalarGridSpec(
            num_scalar_prefetch=1,
            grid=(1,),
            in_specs=[
                whole_spec(parts),
                pl.BlockSpec((2, 1, ints.shape[2]), lambda i, s: (s[rollouts], 0, 0)),
                pl.BlockSpec((rollouts, 1, slots, HD), lambda i, s: (0, s[rollouts + 1], 0, 0)),
                pl.BlockSpec((rollouts, 1, slots, HD), lambda i, s: (0, s[rollouts + 1], 0, 0)),
            ],
            out_specs=[
                pl.BlockSpec((rollouts, steps, HD), lambda *_: (0, 0, 0)),
                pl.BlockSpec((rows_here, w_llama.shape[2]), lambda *_: (0, 0)),
                pl.BlockSpec((rows_here, w_qwen.shape[2]), lambda *_: (0, 0)),
            ],
        ),
        out_shape=[
            jax.ShapeDtypeStruct((rollouts, steps, HD), BF16),
            jax.ShapeDtypeStruct((rows_here, w_llama.shape[2]), BF16),
            jax.ShapeDtypeStruct((rows_here, w_qwen.shape[2]), BF16),
        ],
        name="last",
    )(scalars, parts, ints, cache_keys, cache_values)
    return (attn, llama, qwen)


def solution(mesh):
    return jax.shard_map(
        shards,
        mesh=mesh,
        in_specs=(
            P("dp", None),
            P("dp", "tensor"),
            P("tensor"),
            P("tensor", None),
            P("tensor", None),
            P("dp", None, None, None),
            P("dp", None, None, None),
            P("dp"),
            P("dp", "tensor"),
            P("tensor", None, "dp"),
            P("tensor", None, "dp"),
            P("dp", None),
            P("dp", None),
        ),
        out_specs=(P("dp", None, "tensor"), P("tensor", "dp"), P("tensor", "dp")),
        check_vma=False,
    )
```

time: 397 us -> 96.7 us (0.24)
  blocking collectives: 343 us -> 0 us
  starting transfers between devices: 0.04 us -> 30 us
  waiting for transfers between devices: 16.7 us -> 43.4 us
  between operations: 14.9 us -> 0.69 us
  Pallas kernels: 0 us -> 13.4 us
  matrix products: 5.2 us -> 0 us
  local copies, waits for them, and re-layouts: 9.69 us -> 5.35 us
    all_gather x4 -> x0, blocking collectives: 137 us -> none  [the longest x1 40.1 us: shards(): lax.all_gather(tokens, 'dp', axis=0, tiled=True)]
    unnamed x1 -> x0, blocking collectives: 114 us -> none
    psum x1 -> x0, blocking collectives: 92 us -> none  [shards(): lax.psum((query_part, pair_part, squares), 'tensor')]
    all_to_all x0 -> x3, waiting for transfers between devices: none -> 43.4 us  [the longest x1 18.9 us: shards(): lax.all_to_all(joined, 'tensor', 0, 0, axis_index_groups=lines, tiled=True)]
    all_to_all x0 -> x3, starting transfers between devices: none -> 24.6 us  [the longest x1 13.7 us: shards(): ints = lax.all_to_all(ints, 'dp', 0, 0, tiled=True)]
    psum x1 -> x0, waiting for transfers between devices: 16.7 us -> none  [shards(): lax.psum((query_part, pair_part, squares), 'tensor')]
    pallas_call x0 -> x4, Pallas kernels: none -> 13.4 us  [the longest x2 7.64 us: part(): pl.pallas_call(part_kernel, grid_spec=pltpu.PrefetchScalarGridSpec(num_sc...]
    ppermute x0 -> x1, starting transfers between devices: none -> 5.44 us  [shards(): lax.ppermute(theirs, 'tensor', [(i, i ^ 1) for i in range(targets)])]
  transfers between devices with their start and end apart: 1 -> 4, of which waited for: 1 -> 3; matrix products, arithmetic and copies ran while one was open for 0% -> 2% of each run, Pallas kernels for 0% -> 4%
where the time goes in v1:
time: 96.7 us; the launch traced here: 96.2 us
  waiting for transfers between devices  43.4 us (45%)
  starting transfers between devices  30 us (31%)
  Pallas kernels  13.4 us (14%)
  local copies, waits for them, and re-layouts  5.35 us (6%)
  other arithmetic  3.33 us (3%)
    all_to_all x1, waiting for transfers between devices, shards(): lax.all_to_all(joined, 'tensor', 0, 0, axis_index_groups=lines, tiled=True)  18.9 us
    all_to_all x1, waiting for transfers between devices, shards(): held = lax.all_to_all(sent, 'dp', 0, 0, tiled=True)  16 us
    all_to_all x1, starting transfers between devices, shards(): ints = lax.all_to_all(ints, 'dp', 0, 0, tiled=True)  13.7 us
    all_to_all x1, waiting for transfers between devices, shards(): ints = lax.all_to_all(ints, 'dp', 0, 0, tiled=True)  8.53 us
    pallas_call x2, Pallas kernels, part(): pl.pallas_call(part_kernel, grid_spec=pltpu.PrefetchScalarGridSpec(num_sc...  7.64 us
    all_to_all x1, starting transfers between devices, shards(): lax.all_to_all(joined, 'tensor', 0, 0, axis_index_groups=lines, tiled=True)  6.82 us
    ppermute x1, starting transfers between devices, shards(): lax.ppermute(theirs, 'tensor', [(i, i ^ 1) for i in range(targets)])  5.44 us
    all_to_all x1, starting transfers between devices, shards(): held = lax.all_to_all(sent, 'dp', 0, 0, tiled=True)  4.03 us
  transfers between devices with their start and end apart: 4, of which 3 were waited for; matrix products, arithmetic and copies ran while one was open for 2% of the time, Pallas kernels for 4%

profile of v1, /device:TPU:1, one launch (start us, length us, event | category | flops | bytes accessed | tf_op | source)
XLA Modules:
  0.0 96.2 jit_solution(765395340503067329)
XLA Ops:
  0.6 0.8 reshape.32
  1.4 0.7 add_bitcast_fusion
  2.1 0.6 broadcast_in_dim.9
  2.8 13.7 %all-to-all-start = ((s32[32,1,16]{2,1,0:T(1,128)}), s32[32,1,16]{2,1,0:T(1,128)S(1)}, u32[]{:S(2)}, u32[]{:S(2)}) async-start(s32[32,1,16]{2,1,0:T(1,128)} %broadcast_in_dim.9), calls=%async_computation | async-start | bytes 32768 | tf_op jit(solution)/shard_map/all_to_all | solution.py:186
  16.5 8.5 %all-to-all-done.ints_ref = s32[32,1,16]{2,1,0:T(1,128)S(1)} async-done(((s32[32,1,16]{2,1,0:T(1,128)}), s32[32,1,16]{2,1,0:T(1,128)S(1)}, u32[]{:S(2)}, u32[]{:S(2)}) %all-to-all-start) | async-done | bytes 2080 | tf_op jit(solution)/shard_map/all_to_all | solution.py:186
  25.0 0.0 copy-start.3
  25.0 0.6 copy-done.3
  25.6 2.7 %fetch.1 = bf16[32,16,640]{2,1,0:T(8,128)(2,1)} custom-call(s32[1]{0:T(128)} %bitcast.3.first_ref, s32[32,1,16]{2,1,0:T(1,128)} %copy-done.3, bf16[224,2432]{1,0:T(8,128)(2,1)} %bitcast.22, bf16[16,512]{1,0:T(8,128)(2,1)} %rows_ref.1), custom_call_target="tpu_custom_call" | custom-call | tf_op jit(solution)/shard_map/fetch/pallas_call | solution.py:189
  28.3 0.0 copy-start.5
  28.3 0.0 copy-start.2
  28.3 4.0 %all-to-all-start.1 = ((bf16[32,16,640]{2,1,0:T(8,128)(2,1)}), bf16[32,16,640]{2,1,0:T(8,128)(2,1)S(1)}, u32[]{:S(2)}, u32[]{:S(2)}) async-start(bf16[32,16,640]{2,1,0:T(8,128)(2,1)} %fetch.1), calls=%async_computation.1 | async-start | bytes 1310720 | tf_op jit(solution)/shard_map/all_to_all | solution.py:200
  32.3 0.0 copy-done.5
  32.4 0.6 reshape.35.gain_ref
  32.9 0.0 copy-done.2
  32.9 1.1 %copy.20 = bf16[512,2,462]{0,2,1:T(8,128)(2,1)} copy(bf16[512,2,462]{0,1,2:T(2,128)(2,1)S(1)} %copy-done.2) | data formatting | bytes 1892352 | tf_op args[10]
  34.0 16.0 %all-to-all-done.1.found_ref = bf16[32,16,640]{2,1,0:T(8,128)(2,1)S(1)} async-done(((bf16[32,16,640]{2,1,0:T(8,128)(2,1)}), bf16[32,16,640]{2,1,0:T(8,128)(2,1)S(1)}, u32[]{:S(2)}, u32[]{:S(2)}) %all-to-all-start.1) | async-done | bytes 655392 | tf_op jit(solution)/shard_map/all_to_all | solution.py:200
  50.1 0.0 copy-start
  50.1 0.9 copy-done
  50.9 3.8 %part.2 = bf16[8,32,1152]{2,1,0:T(8,128)(2,1)} custom-call(s32[1]{0:T(128)} %bitcast.2.side_ref, bf16[8,2,32,640]{3,2,1,0:T(8,128)(2,1)} %bitcast.16, bf16[32,16,640]{2,1,0:T(8,128)(2,1)} %copy-done, s32[8,2,2,1,16]{4,3,2,1,0:T(1,128)} %bitcast.23, bf16[1,224]{1,0:T(2,128)(2,1)} %reshape.35.gain_ref, bf16[224,2048]{1,0:T(8,128)(2,1)} %wq_ref.3, ...), custom_call_target="tpu_custom_call" | custom-call | tf_op jit(solution)/shard_map/part/pallas_call | solution.py:211
  54.8 5.4 %collective-permute-start = (bf16[8,32,1152]{2,1,0:T(8,128)(2,1)}, bf16[8,32,1152]{2,1,0:T(8,128)(2,1)S(1)}, u32[]{:S(2)}, u32[]{:S(2)}) collective-permute-start(bf16[8,32,1152]{2,1,0:T(8,128)(2,1)} %part.2), channel_id=1, source_target_pairs={{0,1},{1,0},{2,3},{3,2},{4,5},{5,4},{6,7},{7,6},{8,9},{9,8},{10,11... | collective-permute-start | bytes 1769480 | tf_op jit(solution)/shard_map/ppermute | solution.py:236
  60.2 3.8 %part.3 = bf16[8,32,1152]{2,1,0:T(8,128)(2,1)} custom-call(s32[1]{0:T(128)} %bitcast.11.side_ref, bf16[8,2,32,640]{3,2,1,0:T(8,128)(2,1)} %bitcast.17, bf16[32,16,640]{2,1,0:T(8,128)(2,1)} %copy-done, s32[8,2,2,1,16]{4,3,2,1,0:T(1,128)} %bitcast.24, bf16[1,224]{1,0:T(2,128)(2,1)} %reshape.35.gain_ref, bf16[224,2048]{1,0:T(8,128)(2,1)} %wq_ref.3, ...), custom_call_target="tpu_custom_call" | custom-call | tf_op jit(solution)/shard_map/part/pallas_call | solution.py:211
  64.0 0.0 copy-start.4
  64.0 0.0 collective-permute-done
  64.0 2.0 %add_convert_fusion = bf16[8,32,1152]{2,1,0:T(8,128)(2,1)} fusion(bf16[8,32,1152]{2,1,0:T(8,128)(2,1)} %part.3, bf16[8,32,1152]{2,1,0:T(8,128)(2,1)S(1)} %collective-permute-done), kind=kLoop, calls=%fused_computation | loop fusion | flops 1179648 | bytes 1769472 | tf_op jit(solution)/shard_map/convert_element_type | solution.py:238
  66.1 6.8 %all-to-all-start.2 = ((bf16[8,32,1152]{2,1,0:T(8,128)(2,1)}), bf16[8,32,1152]{2,1,0:T(8,128)(2,1)S(1)}, u32[]{:S(2)}, u32[]{:S(2)}) async-start(bf16[8,32,1152]{2,1,0:T(8,128)(2,1)} %add_convert_fusion), calls=%async_computation.2 | async-start | bytes 1179648 | tf_op jit(solution)/shard_map/all_to_all | solution.py:240
  72.9 0.0 copy-done.4
  72.9 0.6 pad_add_fusion.sizes_ref
  73.5 18.9 %all-to-all-done.2.parts_ref = bf16[8,32,1152]{2,1,0:T(8,128)(2,1)S(1)} async-done(((bf16[8,32,1152]{2,1,0:T(8,128)(2,1)}), bf16[8,32,1152]{2,1,0:T(8,128)(2,1)S(1)}, u32[]{:S(2)}, u32[]{:S(2)}) %all-to-all-start.2) | async-done | bytes 589856 | tf_op jit(solution)/shard_map/all_to_all | solution.py:240
  92.3 0.0 copy-start.1
  92.3 0.8 copy-done.1
  93.1 3.1 %last.1 = (bf16[2,4,128]{2,1,0:T(4,128)(2,1)}, bf16[32,448]{1,0:T(8,128)(2,1)}, bf16[32,462]{1,0:T(8,128)(2,1)}) custom-call(s32[4]{0:T(128)} %pad_add_fusion.sizes_ref, bf16[8,32,1152]{2,1,0:T(8,128)(2,1)} %copy-done.1, s32[32,1,16]{2,1,0:T(1,128)} %copy-done.3, bf16[2,4,64,128]{3,2,1,0:T(8,128)(2,1)} %keys_ref.1, bf16[2,4,64,128]{3,2,1,0:T(8,128)(2,1)} %values_ref.1), custom_call_target="tpu_custom_call" | custom-call | tf_op jit(solution)/shard_map/last/pallas_call | solution.py:247
Async XLA Ops:
  2.8 22.2 %all-to-all-start = ((s32[32,1,16]{2,1,0:T(1,128)}), s32[32,1,16]{2,1,0:T(1,128)S(1)}, u32[]{:S(2)}, u32[]{:S(2)}) async-start(s32[32,1,16]{2,1,0:T(1,128)} %broadcast_in_dim.9), calls=%async_computation | async-start | bytes 32768 | tf_op jit(solution)/shard_map/all_to_all | solution.py:186
  25.0 0.6 copy-start.3
  28.3 4.1 %copy-start.5 = (bf16[224]{0:T(256)(128)(2,1)S(1)}, bf16[224]{0:T(256)(128)(2,1)}, u32[]{:S(2)}) copy-start(bf16[224]{0:T(256)(128)(2,1)} %param.15) | copy-start | bytes 1348
  28.3 4.6 %copy-start.2 = (bf16[512,2,462]{0,1,2:T(2,128)(2,1)S(1)}, bf16[512,2,462]{0,1,2:T(2,128)(2,1)}, u32[]{:S(2)}) copy-start(bf16[512,2,462]{0,1,2:T(2,128)(2,1)} %param.23) | copy-start | bytes 2838532
  28.3 21.8 %all-to-all-start.1 = ((bf16[32,16,640]{2,1,0:T(8,128)(2,1)}), bf16[32,16,640]{2,1,0:T(8,128)(2,1)S(1)}, u32[]{:S(2)}, u32[]{:S(2)}) async-start(bf16[32,16,640]{2,1,0:T(8,128)(2,1)} %fetch.1), calls=%async_computation.1 | async-start | bytes 1310720 | tf_op jit(solution)/shard_map/all_to_all | solution.py:200
  50.1 0.9 copy-start
  54.8 9.3 %collective-permute-start = (bf16[8,32,1152]{2,1,0:T(8,128)(2,1)}, bf16[8,32,1152]{2,1,0:T(8,128)(2,1)S(1)}, u32[]{:S(2)}, u32[]{:S(2)}) collective-permute-start(bf16[8,32,1152]{2,1,0:T(8,128)(2,1)} %part.2), channel_id=1, source_target_pairs={{0,1},{1,0},{2,3},{3,2},{4,5},{5,4},{6,7},{7,6},{8,9},{9,8},{10,11... | collective-permute-start | bytes 1769480 | tf_op jit(solution)/shard_map/ppermute | solution.py:236
  64.0 8.9 %copy-start.4 = (s32[2]{0:T(128)S(1)}, s32[2]{0:T(128)}, u32[]{:S(2)}) copy-start(s32[2]{0:T(128)} %param.20) | copy-start | bytes 28
  66.1 26.3 %all-to-all-start.2 = ((bf16[8,32,1152]{2,1,0:T(8,128)(2,1)}), bf16[8,32,1152]{2,1,0:T(8,128)(2,1)S(1)}, u32[]{:S(2)}, u32[]{:S(2)}) async-start(bf16[8,32,1152]{2,1,0:T(8,128)(2,1)} %add_convert_fusion), calls=%async_computation.2 | async-start | bytes 1179648 | tf_op jit(solution)/shard_map/all_to_all | solution.py:240
  92.3 0.8 copy-start.1

commit v2 on v1

v2 whole, which is shorter than its diff:
```python
import math

import jax
import jax.numpy as jnp
from jax import lax
from jax.experimental import pallas as pl
from jax.experimental.pallas import tpu as pltpu
from jax.sharding import PartitionSpec as P

DS = 3584
HD = 128
KVH = 4
EPS = 1e-06
F32 = jnp.float32
BF16 = jnp.bfloat16
VMEM_LIMIT = 28 * 2**20


def nt_dot(a, b):
    return lax.dot_general(a, b, (((1,), (1,)), ((), ())), preferred_element_type=F32)


def pack_kernel(tokens_ref, lens_ref, kinds_ref, rows_ref, out_ref):
    groups, count, _ = out_ref.shape
    width = rows_ref.shape[1]
    steps = tokens_ref.shape[1]
    lane = lax.broadcasted_iota(jnp.int32, (count, HD), 1)
    sub = lax.broadcasted_iota(jnp.int32, (count, HD), 0)
    info = jnp.zeros((count, HD), jnp.int32)
    for s in range(tokens_ref.shape[0] * steps):
        token = tokens_ref[s // steps, s % steps]
        digits = jnp.where(
            lane == 0, token >> 12, jnp.where(lane == 1, (token >> 6) & 63, token & 63)
        )
        info = jnp.where(jnp.logical_and(sub == s, lane < 3), digits, info)
    one = lens_ref[0, 0]
    two = one + lens_ref[0, 1]
    three = two + lens_ref[0, 2]
    owner = jnp.where(
        sub < one,
        kinds_ref[0, 0],
        jnp.where(sub < two, kinds_ref[0, 1], jnp.where(sub < three, kinds_ref[0, 2], kinds_ref[0, 3])),
    )
    info = jnp.where(lane == 3, owner, info).astype(F32).astype(BF16)
    out_ref[:, :, :width] = jnp.broadcast_to(rows_ref[...][None], (groups, count, width))
    out_ref[:, :, width:] = jnp.broadcast_to(info[None], (groups, count, HD))


def fetch_kernel(first_ref, info_ref, table_ref, out_ref):
    groups, per, padded = out_ref.shape
    columns, vocab = table_ref.shape
    info = info_ref[...].astype(F32)[:, :per]
    ids = info[:, :, 0:1] * 4096.0 + info[:, :, 1:2] * 64.0 + info[:, :, 2:3]
    ids = ids.astype(jnp.int32).reshape(groups * per, 1) - first_ref[0]
    place = lax.broadcasted_iota(jnp.int32, (groups * per, vocab), 1)
    hot = jnp.where(ids == place, 1.0, 0.0).astype(BF16)
    found = nt_dot(hot, table_ref[...])
    found = jnp.concatenate([found, jnp.zeros((groups * per, padded - columns), F32)], axis=1)
    out_ref[...] = found.astype(BF16).reshape(groups, per, padded)


def teacher_kernel(side_ref, rows_ref, info_ref, wl_ref, ww_ref, *rest):
    out_ref = rest[-1]
    places, _, count, width = rows_ref.shape
    half = wl_ref.shape[1]
    wide = ww_ref.shape[1]
    padded = -(-wide // HD) * HD
    rows = rows_ref[...].reshape(places * count, width)
    info = info_ref[...].astype(F32).reshape(places * count, HD)
    first = info[:, 3:4] == 0.0
    for k in range(2):
        one = nt_dot(rows, wl_ref[k])
        two = nt_dot(rows, ww_ref[k])
        one = jnp.concatenate([one, jnp.zeros((places * count, padded - half), F32)], axis=1)
        two = jnp.concatenate([two, jnp.zeros((places * count, padded - wide), F32)], axis=1)
        both = jnp.where(first, one, two).reshape(places, count, padded)
        if len(rest) > 1:
            both = both + rest[0][:, :, k * padded : (k + 1) * padded].astype(F32)
        out_ref[:, :, k * padded : (k + 1) * padded] = both.astype(BF16)


def student_kernel(side_ref, found_ref, gain_ref, wq_ref, wkv_ref, own_ref, other_ref, query_ref):
    places = own_ref.shape[0]
    per = found_ref.shape[1]
    columns = wq_ref.shape[0]
    x = jnp.sum(found_ref[...].astype(F32), axis=0)[:, :columns]
    scaled = (x * gain_ref[...].astype(F32).reshape(1, columns)).astype(BF16)
    query_ref[...] = jnp.dot(scaled, wq_ref[...], preferred_element_type=F32)
    pair = jnp.dot(scaled, wkv_ref[...], preferred_element_type=F32)
    squares = jnp.broadcast_to(jnp.sum(x * x, axis=1, keepdims=True), (per, HD))
    for out_ref, side in ((own_ref, side_ref[0]), (other_ref, 1 - side_ref[0])):
        for p in range(places):
            head = p * KVH // places
            start = pl.multiple_of((2 * p + side) * HD, HD)
            out_ref[p, :per] = query_ref[:, pl.ds(start, HD)]
            out_ref[p, per : 2 * per] = pair[:, head * HD : (head + 1) * HD]
            out_ref[p, 2 * per : 3 * per] = pair[:, (KVH + head) * HD : (KVH + head + 1) * HD]
            out_ref[p, 3 * per :] = squares


def last_kernel(
    place_ref, sizes_ref, parts_ref, info_ref, keys_ref, values_ref, attn_ref, llama_ref, qwen_ref
):
    half = llama_ref.shape[1]
    wide = qwen_ref.shape[1]
    padded = (parts_ref.shape[2] - HD) // 2
    total = jnp.sum(parts_ref[...].astype(F32), axis=0)
    gate = total[:, :padded]
    hidden = gate / (1.0 + jnp.exp(-gate)) * total[:, padded : 2 * padded]
    first = info_ref[0].astype(F32)[:, 3:4] == 0.0
    llama_ref[...] = jnp.where(first, hidden, 0.0)[:, :half].astype(BF16)
    qwen_ref[...] = jnp.where(first, 0.0, hidden)[:, :wide].astype(BF16)

    rollouts, _, slots, _ = keys_ref.shape
    per = parts_ref.shape[1] // 4
    steps = per // rollouts
    student = total[:, 2 * padded :]
    inverse = lax.rsqrt(student[3 * per :] / DS + EPS)
    query = (student[:per] * inverse).astype(BF16)
    key = (student[per : 2 * per] * inverse).astype(BF16)
    value = (student[2 * per : 3 * per] * inverse).astype(BF16)
    scale = 1.0 / math.sqrt(HD)
    score_new = nt_dot(query, key) * scale
    row = lax.broadcasted_iota(jnp.int32, (per, per), 0)
    col = lax.broadcasted_iota(jnp.int32, (per, per), 1)
    fits = jnp.logical_and(row // steps == col // steps, col <= row)
    score_new = jnp.where(fits, score_new, -jnp.inf)
    for b in range(rollouts):
        score = nt_dot(query, keys_ref[b, 0]) * scale
        slot = lax.broadcasted_iota(jnp.int32, (per, slots), 1)
        score = jnp.where(slot < sizes_ref[b], score, -jnp.inf)
        mine = score_new[b * steps : (b + 1) * steps]
        score = score[b * steps : (b + 1) * steps]
        top = jnp.maximum(
            jnp.max(score, axis=1, keepdims=True), jnp.max(mine, axis=1, keepdims=True)
        )
        old_exp = jnp.exp(score - top)
        new_exp = jnp.exp(mine - top)
        whole = jnp.sum(old_exp, axis=1, keepdims=True) + jnp.sum(new_exp, axis=1, keepdims=True)
        old = (old_exp / whole).astype(BF16)
        new = (new_exp / whole).astype(BF16)
        mixed = jnp.dot(old, values_ref[b, 0], preferred_element_type=F32)
        mixed = mixed + jnp.dot(new, value, preferred_element_type=F32)
        attn_ref[b] = mixed.astype(BF16)


def near(array):
    return pltpu.with_memory_space_constraint(array, pltpu.VMEM)


def far(array):
    return pltpu.with_memory_space_constraint(array, pltpu.HBM)


def whole_spec(array):
    rank = len(array.shape)
    return pl.BlockSpec(array.shape, lambda *_: (0,) * rank)


def call(kernel, scalars, operands, in_specs, outs, keep=True):
    return pl.pallas_call(
        kernel,
        grid_spec=pltpu.PrefetchScalarGridSpec(
            num_scalar_prefetch=len(scalars),
            grid=(1,),
            in_specs=in_specs,
            out_specs=[whole_spec(out) for out in outs],
        ),
        out_shape=[pltpu.VMEM(o.shape, o.dtype) for o in outs] if keep else outs,
        compiler_params=pltpu.CompilerParams(vmem_limit_bytes=VMEM_LIMIT),
    )(*scalars, *operands)


def shards(
    tokens,
    embed_table,
    norm_gain,
    w_query,
    w_key_value,
    cache_keys,
    cache_values,
    cache_len,
    teacher_rows,
    w_llama,
    w_qwen,
    rollout_len,
    teacher_of,
):
    groups = lax.axis_size("dp")
    targets = lax.axis_size("tensor")
    places = targets // 2
    tensor_index = lax.axis_index("tensor")
    rollouts, steps = tokens.shape
    per = rollouts * steps
    vocab, columns = embed_table.shape
    count, width = teacher_rows.shape
    rows_here = groups * count // targets
    padded = -(-columns // HD) * HD
    half_pad = -(-w_qwen.shape[2] // HD) * HD
    shape = jax.ShapeDtypeStruct
    block = width // HD

    first = (lax.axis_index("dp") * vocab).reshape(1)
    core = (tensor_index & 1).reshape(1)
    other = 1 - core
    place = jnp.stack([tensor_index, lax.div(tensor_index * KVH, targets)])

    (held,) = call(
        pack_kernel,
        [far(tokens), far(rollout_len), far(teacher_of)],
        [far(teacher_rows)],
        [whole_spec(teacher_rows)],
        [shape((groups, count, width + HD), BF16)],
    )
    held, first, core, other, place = lax.optimization_barrier((held, first, core, other, place))
    held = lax.all_to_all(held, "dp", 0, 0, tiled=True)
    held, norm_gain, cache_len, w_qwen = lax.optimization_barrier(
        (held, norm_gain, cache_len, w_qwen)
    )

    table = embed_table.T
    (found,) = call(
        fetch_kernel,
        [first],
        [near(held), near(table)],
        [
            pl.BlockSpec((groups, count, HD), lambda i, s: (0, 0, block)),
            whole_spec(table),
        ],
        [shape((groups, per, padded), BF16)],
    )
    found = lax.all_to_all(found, "dp", 0, 0, tiled=True)

    by_place = near(held.reshape(places, 2, rows_here, width + HD))
    first_w = near(jnp.transpose(w_llama, (1, 2, 0)))
    second_w = near(jnp.transpose(w_qwen, (1, 2, 0)))

    def teacher(side, extra, width_out):
        return call(
            teacher_kernel,
            [side],
            [by_place, by_place, first_w, second_w, *extra],
            [
                pl.BlockSpec((places, 1, rows_here, width), lambda i, s: (0, s[0], 0, 0)),
                pl.BlockSpec((places, 1, rows_here, HD), lambda i, s: (0, s[0], 0, block)),
                whole_spec(first_w),
                whole_spec(second_w),
                *[whole_spec(a) for a in extra],
            ],
            [shape((places, rows_here, width_out), BF16)],
        )[0]

    pairs = [(i, i ^ 1) for i in range(targets)]
    theirs = teacher(other, [], 2 * half_pad)
    theirs = lax.ppermute(theirs, "tensor", pairs)
    joined = teacher(core, [near(theirs)], 2 * half_pad + HD)

    gain = norm_gain
    found, joined, gain = lax.optimization_barrier((found, joined, gain))
    ours, theirs = pl.pallas_call(
        student_kernel,
        grid_spec=pltpu.PrefetchScalarGridSpec(
            num_scalar_prefetch=1,
            grid=(1,),
            in_specs=[whole_spec(a) for a in (found, gain, w_query, w_key_value)],
            out_specs=[pl.BlockSpec((places, 4 * per, HD), lambda *_: (0, 0, 0))] * 2,
            scratch_shapes=[pltpu.VMEM((per, w_query.shape[1]), F32)],
        ),
        out_shape=[pltpu.VMEM((places, 4 * per, HD), F32)] * 2,
        name="student",
        compiler_params=pltpu.CompilerParams(vmem_limit_bytes=VMEM_LIMIT),
    )(core, near(found), gain, far(w_query), far(w_key_value))
    theirs = lax.ppermute(theirs, "tensor", pairs)
    joined = lax.dynamic_update_slice(joined, (ours + theirs).astype(BF16), (0, 0, 2 * half_pad))

    lines = [[2 * p + c for p in range(places)] for c in range(2)]
    joined, place, cache_len = lax.optimization_barrier((joined, place, cache_len))
    parts = lax.all_to_all(joined, "tensor", 0, 0, axis_index_groups=lines, tiled=True)
    parts, place, cache_len = lax.optimization_barrier((parts, place, cache_len))

    by_target = held.reshape(targets, rows_here, width + HD)
    slots = cache_keys.shape[2]
    cache_spec = pl.BlockSpec((rollouts, 1, slots, HD), lambda i, s, _: (0, s[1], 0, 0))
    return tuple(call(
        last_kernel,
        [place, cache_len],
        [near(parts), near(by_target), cache_keys, cache_values],
        [
            whole_spec(parts),
            pl.BlockSpec((1, rows_here, HD), lambda i, s, _: (s[0], 0, block)),
            cache_spec,
            cache_spec,
        ],
        [
            shape((rollouts, steps, HD), BF16),
            shape((rows_here, w_llama.shape[2]), BF16),
            shape((rows_here, w_qwen.shape[2]), BF16),
        ],
        keep=False,
    ))


def solution(mesh):
    return jax.shard_map(
        shards,
        mesh=mesh,
        in_specs=(
            P("dp", None),
            P("dp", "tensor"),
            P("tensor"),
            P("tensor", None),
            P("tensor", None),
            P("dp", None, None, None),
            P("dp", None, None, None),
            P("dp"),
            P("dp", "tensor"),
            P("tensor", None, "dp"),
            P("tensor", None, "dp"),
            P("dp", None),
            P("dp", None),
        ),
        out_specs=(P("dp", None, "tensor"), P("tensor", "dp"), P("tensor", "dp")),
        check_vma=False,
    )
```

time: 96.7 us -> 91 us (0.941)
  blocking collectives: 0 us -> 57.2 us
  waiting for transfers between devices: 43.4 us -> 8.29 us
  starting transfers between devices: 30 us -> 12.6 us
  Pallas kernels: 13.4 us -> 8.64 us
  other arithmetic: 3.33 us -> 0.1 us
  local copies, waits for them, and re-layouts: 5.35 us -> 3.03 us
    all_to_all x0 -> x2, blocking collectives: none -> 57.2 us  [the longest x1 32.2 us: shards(): held = lax.all_to_all(held, 'dp', 0, 0, tiled=True)]
    all_to_all x3 -> x1, waiting for transfers between devices: 43.4 us -> 7.32 us  [shards(): found = lax.all_to_all(found, 'dp', 0, 0, tiled=True)]
    all_to_all x3 -> x1, starting transfers between devices: 24.6 us -> 4.71 us  [shards(): found = lax.all_to_all(found, 'dp', 0, 0, tiled=True)]
    pallas_call x4 -> x6, Pallas kernels: 13.4 us -> 8.64 us  [the longest x5 7.04 us: call(): pl.pallas_call(kernel, grid_spec=pltpu.PrefetchScalarGridSpec(num_scalar_...]
    ppermute x1 -> x2, starting transfers between devices: 5.44 us -> 7.86 us  [shards(): theirs = lax.ppermute(theirs, 'tensor', pairs)]
    convert_element_type x1 -> x0, other arithmetic: 2.02 us -> none  [shards(): joined = (theirs.astype(F32) + ours.astype(F32)).astype(BF16)]
    reshape x2 -> x0, local copies, waits for them, and re-layouts: 1.33 us -> none  [the longest x1 0.76 us: shards(): tokens.reshape(1, per)]
    unnamed x13 -> x18, local copies, waits for them, and re-layouts: 3.41 us -> 2.89 us
  transfers between devices with their start and end apart: 4 -> 3, of which waited for: 3 -> 2; matrix products, arithmetic and copies ran while one was open for 2% -> 0% of each run, Pallas kernels for 4% -> 2%
where the time goes in v2:
time: 91 us; the launch traced here: 90.6 us
  blocking collectives  57.2 us (63%)
  starting transfers between devices  12.6 us (14%)
  Pallas kernels  8.64 us (9%)
  waiting for transfers between devices  8.29 us (9%)
  local copies, waits for them, and re-layouts  3.03 us (3%)
    all_to_all x1, blocking collectives, shards(): held = lax.all_to_all(held, 'dp', 0, 0, tiled=True)  32.2 us
    all_to_all x1, blocking collectives, shards(): lax.all_to_all(joined, 'tensor', 0, 0, axis_index_groups=lines, tiled=True)  25 us
    ppermute x2, starting transfers between devices, shards(): theirs = lax.ppermute(theirs, 'tensor', pairs)  7.86 us
    all_to_all x1, waiting for transfers between devices, shards(): found = lax.all_to_all(found, 'dp', 0, 0, tiled=True)  7.32 us
    pallas_call x5, Pallas kernels, call(): pl.pallas_call(kernel, grid_spec=pltpu.PrefetchScalarGridSpec(num_scalar_...  7.04 us
    all_to_all x1, starting transfers between devices, shards(): found = lax.all_to_all(found, 'dp', 0, 0, tiled=True)  4.71 us
    unnamed x18, local copies, waits for them, and re-layouts  2.89 us
  transfers between devices with their start and end apart: 3, of which 2 were waited for; matrix products, arithmetic and copies ran while one was open for 0% of the time, Pallas kernels for 2%

profile of v2, /device:TPU:1, one launch (start us, length us, event | category | flops | bytes accessed | tf_op | source)
XLA Modules:
  0.0 90.6 jit_solution(6763705123749991479)
XLA Ops:
  0.6 0.1 pad_add_fusion.place_ref
  0.7 0.0 copy-start.8
  0.7 1.6 %shard_map.148 = bf16[32,16,640]{2,1,0:T(8,128)(2,1)S(1)} custom-call(s32[2,4]{1,0:T(2,128)} %tokens_ref.1, s32[1,4]{1,0:T(1,128)} %lens_ref.1, s32[1,4]{1,0:T(1,128)} %kinds_ref.1, bf16[16,512]{1,0:T(8,128)(2,1)} %rows_ref.1), custom_call_target="tpu_custom_call" | custom-call | tf_op jit(solution)/shard_map/pallas_call | solution.py:161
  2.3 32.2 %all_to_all.15.info_ref = bf16[32,16,640]{2,1,0:T(8,128)(2,1)S(1)} all-to-all(bf16[32,16,640]{2,1,0:T(8,128)(2,1)S(1)} %shard_map.148), channel_id=1, replica_groups=mesh['dp'=32,'tensor'=16] {'dp'}, dimensions={0} | all-to-all | bytes 1310720 | tf_op jit(solution)/shard_map/all_to_all | solution.py:216
  34.5 0.0 copy-done.8
  34.5 0.0 copy-start
  34.5 0.1 copy.18
  34.6 1.0 %copy-done = bf16[512,2,448]{0,2,1:T(8,128)(2,1)S(1)} copy-done((bf16[512,2,448]{0,2,1:T(8,128)(2,1)S(1)}, bf16[512,2,448]{0,2,1:T(8,128)(2,1)}, u32[]{:S(2)}) %copy-start) | copy-done | bytes 917528
  35.7 0.0 copy-start.1
  35.7 1.5 %shard_map.150 = bf16[8,32,1024]{2,1,0:T(8,128)(2,1)} custom-call(s32[1]{0:T(128)S(6)} %sub.3.side_ref, bf16[8,2,32,640]{3,2,1,0:T(8,128)(2,1)S(1)} %bitcast.11, bf16[8,2,32,640]{3,2,1,0:T(8,128)(2,1)S(1)} %bitcast.12, bf16[2,448,512]{2,1,0:T(8,128)(2,1)S(1)} %bitcast.18, bf16[2,462,512]{2,1,0:T(8,128)(2,1)S(1)} %bitcast.16), custom_call_target="tpu_custom_call" | custom-call | tf_op jit(solution)/shard_map/pallas_call | solution.py:161
  37.2 4.4 %collective-permute-start = (bf16[8,32,1024]{2,1,0:T(8,128)(2,1)}, bf16[8,32,1024]{2,1,0:T(8,128)(2,1)S(1)}, u32[]{:S(2)}, u32[]{:S(2)}) collective-permute-start(bf16[8,32,1024]{2,1,0:T(8,128)(2,1)} %shard_map.150), channel_id=1, source_target_pairs={{0,1},{1,0},{2,3},{3,2},{4,5},{5,4},{6,7},{7,6},{8,9},{9,8},{10,11... | collective-permute-start | bytes 1572872 | tf_op jit(solution)/shard_map/ppermute | solution.py:255
  41.6 0.0 copy-done.1
  41.6 1.3 %shard_map.149 = bf16[32,8,256]{2,1,0:T(8,128)(2,1)} custom-call(s32[1]{0:T(128)} %bitcast.first_ref, bf16[32,16,640]{2,1,0:T(8,128)(2,1)S(1)} %all_to_all.15.info_ref, bf16[224,2432]{1,0:T(8,128)(2,1)S(1)} %bitcast.20), custom_call_target="tpu_custom_call" | custom-call | tf_op jit(solution)/shard_map/pallas_call | solution.py:161
  42.9 4.7 %all-to-all-start.1 = ((bf16[32,8,256]{2,1,0:T(8,128)(2,1)}), bf16[32,8,256]{2,1,0:T(8,128)(2,1)S(1)}, u32[]{:S(2)}, u32[]{:S(2)}) async-start(bf16[32,8,256]{2,1,0:T(8,128)(2,1)} %shard_map.149), calls=%async_computation.1 | async-start | bytes 262144 | tf_op jit(solution)/shard_map/all_to_all | solution.py:232
  47.6 0.0 collective-permute-done.rest_0_
  47.7 0.0 copy-start.2
  47.7 0.8 copy-done.2
  48.4 0.0 copy-start.3
  48.5 1.0 %copy-done.3 = bf16[8,32,1024]{2,1,0:T(8,128)(2,1)S(1)} copy-done((bf16[8,32,1024]{2,1,0:T(8,128)(2,1)S(1)}, bf16[8,32,1024]{2,1,0:T(8,128)(2,1)}, u32[]{:S(2)}) %copy-start.3) | copy-done | bytes 524312
  49.5 0.0 copy-start.6
  49.5 0.7 shard_map.151
  50.2 7.3 %all-to-all-done.1.found_ref = bf16[32,8,256]{2,1,0:T(8,128)(2,1)S(1)} async-done(((bf16[32,8,256]{2,1,0:T(8,128)(2,1)}), bf16[32,8,256]{2,1,0:T(8,128)(2,1)S(1)}, u32[]{:S(2)}, u32[]{:S(2)}) %all-to-all-start.1) | async-done | bytes 131104 | tf_op jit(solution)/shard_map/all_to_all | solution.py:232
  57.6 0.0 copy-done.6
  57.6 1.6 %student.1 = (f32[8,32,128]{2,1,0:T(8,128)S(1)}, f32[8,32,128]{2,1,0:T(8,128)S(1)}) custom-call(s32[1]{0:T(128)} %bitcast.1.side_ref, bf16[32,8,256]{2,1,0:T(8,128)(2,1)S(1)} %all-to-all-done.1.found_ref, bf16[224]{0:T(256)(128)(2,1)S(1)} %copy-done.6, bf16[224,2048]{1,0:T(8,128)(2,1)} %wq_ref.1, bf16[224,1024]{1,0:T(8,128)(2,1)} %wkv_ref.1), custom_call_target="tpu_custom_call" | custom-call | tf_op jit(solution)/shard_map/student/pallas_call | solution.py:260
  59.2 0.0 copy-start.4
  59.2 0.0 copy-start.5
  59.2 0.0 copy-start.7
  59.2 3.5 %collective-permute-start.1 = (f32[8,32,128]{2,1,0:T(8,128)S(1)}, f32[8,32,128]{2,1,0:T(8,128)S(1)}, u32[]{:S(2)}, u32[]{:S(2)}) collective-permute-start(f32[8,32,128]{2,1,0:T(8,128)S(1)} %get-tuple-element.34), channel_id=1, source_target_pairs={{0,1},{1,0},{2,3},{3,2},{4,5},{5,4},{6,7},{7,6},{8,9},{9,8},{10,11... | collective-permute-start | bytes 393224 | tf_op jit(solution)/shard_map/ppermute | solution.py:273
  62.7 1.0 %collective-permute-done.1 = f32[8,32,128]{2,1,0:T(8,128)S(1)} collective-permute-done((f32[8,32,128]{2,1,0:T(8,128)S(1)}, f32[8,32,128]{2,1,0:T(8,128)S(1)}, u32[]{:S(2)}, u32[]{:S(2)}) %collective-permute-start.1) | collective-permute-done | bytes 131104 | tf_op jit(solution)/shard_map/ppermute | solution.py:273
  63.7 25.0 %all_to_all.16.parts_ref = bf16[8,32,1152]{2,1,0:T(8,128)(2,1)S(1)} all-to-all(bf16[8,32,1152]{2,1,0:T(8,128)(2,1)S(1)} %fusion), channel_id=1, replica_groups={{0,2,4,6,8,10,12,14},{1,3,5,7,9,11,13,15},{16,18,20,22,24,26,28,30},{17..., dimensions={0} | all-to-all | bytes 1179648 | tf_op jit(solution)/shard_map/all_to_all | solution.py:278
  88.7 0.0 copy-done.4
  88.7 0.0 copy-done.5
  88.7 0.0 copy-done.7
  88.7 1.9 %shard_map.152 = (bf16[2,4,128]{2,1,0:T(4,128)(2,1)}, bf16[32,448]{1,0:T(8,128)(2,1)}, bf16[32,462]{1,0:T(8,128)(2,1)}) custom-call(s32[2]{0:T(128)S(1)} %pad_add_fusion.place_ref, s32[2]{0:T(128)S(1)} %copy-done.7, bf16[8,32,1152]{2,1,0:T(8,128)(2,1)S(1)} %all_to_all.16.parts_ref, bf16[16,32,640]{2,1,0:T(8,128)(2,1)S(1)} %bitcast.15, ...), custom_call_target="tpu_custom_call" | custom-call | tf_op jit(solution)/shard_map/pallas_call | solution.py:161
  (1 shorter events, 0.0 us)
Async XLA Ops:
  0.7 33.8 %copy-start.8 = (bf16[512,2,462]{0,1,2:T(2,128)(2,1)S(1)}, bf16[512,2,462]{0,1,2:T(2,128)(2,1)}, u32[]{:S(2)}) copy-start(bf16[512,2,462]{0,1,2:T(2,128)(2,1)} %param.23) | copy-start | bytes 2838532
  34.5 1.2 %copy-start = (bf16[512,2,448]{0,2,1:T(8,128)(2,1)S(1)}, bf16[512,2,448]{0,2,1:T(8,128)(2,1)}, u32[]{:S(2)}) copy-start(bf16[512,2,448]{0,2,1:T(8,128)(2,1)} %param.22) | copy-start | bytes 2752516
  35.7 5.9 %copy-start.1 = (bf16[2432,224]{0,1:T(8,128)(2,1)S(1)}, bf16[2432,224]{0,1:T(8,128)(2,1)}, u32[]{:S(2)}) copy-start(bf16[2432,224]{0,1:T(8,128)(2,1)} %param.14) | copy-start | bytes 3268612
  37.2 10.4 %collective-permute-start = (bf16[8,32,1024]{2,1,0:T(8,128)(2,1)}, bf16[8,32,1024]{2,1,0:T(8,128)(2,1)S(1)}, u32[]{:S(2)}, u32[]{:S(2)}) collective-permute-start(bf16[8,32,1024]{2,1,0:T(8,128)(2,1)} %shard_map.150), channel_id=1, source_target_pairs={{0,1},{1,0},{2,3},{3,2},{4,5},{5,4},{6,7},{7,6},{8,9},{9,8},{10,11... | collective-permute-start | bytes 1572872 | tf_op jit(solution)/shard_map/ppermute | solution.py:255
  42.9 14.6 %all-to-all-start.1 = ((bf16[32,8,256]{2,1,0:T(8,128)(2,1)}), bf16[32,8,256]{2,1,0:T(8,128)(2,1)S(1)}, u32[]{:S(2)}, u32[]{:S(2)}) async-start(bf16[32,8,256]{2,1,0:T(8,128)(2,1)} %shard_map.149), calls=%async_computation.1 | async-start | bytes 262144 | tf_op jit(solution)/shard_map/all_to_all | solution.py:232
  47.7 0.8 copy-start.2
  48.4 1.0 %copy-start.3 = (bf16[8,32,1024]{2,1,0:T(8,128)(2,1)S(1)}, bf16[8,32,1024]{2,1,0:T(8,128)(2,1)}, u32[]{:S(2)}) copy-start(bf16[8,32,1024]{2,1,0:T(8,128)(2,1)} %copy-done.2) | copy-start | bytes 1572868
  49.5 8.1 %copy-start.6 = (bf16[224]{0:T(256)(128)(2,1)S(1)}, bf16[224]{0:T(256)(128)(2,1)}, u32[]{:S(2)}) copy-start(bf16[224]{0:T(256)(128)(2,1)} %gain_ref) | copy-start | bytes 1348
  59.2 29.5 %copy-start.4 = (bf16[2,4,64,128]{3,2,1,0:T(8,128)(2,1)S(1)}, bf16[2,4,64,128]{3,2,1,0:T(8,128)(2,1)}, u32[]{:S(2)}) copy-start(bf16[2,4,64,128]{3,2,1,0:T(8,128)(2,1)} %keys_ref.1) | copy-start | bytes 393220
  59.2 29.5 %copy-start.5 = (bf16[2,4,64,128]{3,2,1,0:T(8,128)(2,1)S(1)}, bf16[2,4,64,128]{3,2,1,0:T(8,128)(2,1)}, u32[]{:S(2)}) copy-start(bf16[2,4,64,128]{3,2,1,0:T(8,128)(2,1)} %values_ref.1) | copy-start | bytes 393220
  59.2 29.5 %copy-start.7 = (s32[2]{0:T(128)S(1)}, s32[2]{0:T(128)}, u32[]{:S(2)}) copy-start(s32[2]{0:T(128)} %sizes_ref) | copy-start | bytes 28
  59.2 4.4 %collective-permute-start.1 = (f32[8,32,128]{2,1,0:T(8,128)S(1)}, f32[8,32,128]{2,1,0:T(8,128)S(1)}, u32[]{:S(2)}, u32[]{:S(2)}) collective-permute-start(f32[8,32,128]{2,1,0:T(8,128)S(1)} %get-tuple-element.34), channel_id=1, source_target_pairs={{0,1},{1,0},{2,3},{3,2},{4,5},{5,4},{6,7},{7,6},{8,9},{9,8},{10,11... | collective-permute-start | bytes 393224 | tf_op jit(solution)/shard_map/ppermute | solution.py:273

commit v3 on v2

--- a/solution.py
+++ b/solution.py
@@ -13,6 +13,7 @@
 EPS = 1e-06
 F32 = jnp.float32
 BF16 = jnp.bfloat16
+SPARE = 48
 VMEM_LIMIT = 28 * 2**20
 
 
@@ -21,12 +22,14 @@
 
 
 def pack_kernel(tokens_ref, lens_ref, kinds_ref, rows_ref, out_ref):
-    groups, count, _ = out_ref.shape
+    groups = out_ref.shape[0]
+    count = rows_ref.shape[0]
     width = rows_ref.shape[1]
     steps = tokens_ref.shape[1]
-    lane = lax.broadcasted_iota(jnp.int32, (count, HD), 1)
-    sub = lax.broadcasted_iota(jnp.int32, (count, HD), 0)
-    info = jnp.zeros((count, HD), jnp.int32)
+    per = tokens_ref.shape[0] * steps
+    lane = lax.broadcasted_iota(jnp.int32, (per, HD), 1)
+    sub = lax.broadcasted_iota(jnp.int32, (per, HD), 0)
+    info = jnp.zeros((per, HD), jnp.int32)
     for s in range(tokens_ref.shape[0] * steps):
         token = tokens_ref[s // steps, s % steps]
         digits = jnp.where(
@@ -36,20 +39,34 @@
     one = lens_ref[0, 0]
     two = one + lens_ref[0, 1]
     three = two + lens_ref[0, 2]
-    owner = jnp.where(
-        sub < one,
-        kinds_ref[0, 0],
-        jnp.where(sub < two, kinds_ref[0, 1], jnp.where(sub < three, kinds_ref[0, 2], kinds_ref[0, 3])),
-    )
-    info = jnp.where(lane == 3, owner, info).astype(F32).astype(BF16)
-    out_ref[:, :, :width] = jnp.broadcast_to(rows_ref[...][None], (groups, count, width))
-    out_ref[:, :, width:] = jnp.broadcast_to(info[None], (groups, count, HD))
+    for half in range(count // per):
+        row = sub + half * per
+        owner = jnp.where(
+            row < one,
+            kinds_ref[0, 0],
+            jnp.where(
+                row < two, kinds_ref[0, 1], jnp.where(row < three, kinds_ref[0, 2], kinds_ref[0, 3])
+            ),
+        )
+        info = jnp.where(lane == 3 + half, owner, info)
+    rows = rows_ref[...]
+    for k in range(width // HD):
+        piece = rows[:, k * HD : (k + 1) * HD]
+        out_ref[:, k * count : (k + 1) * count] = jnp.broadcast_to(piece[None], (groups, count, HD))
+    info = info.astype(F32).astype(BF16)
+    out_ref[:, width // HD * count :] = jnp.broadcast_to(info[None], (groups, per, HD))
+
+
+def owners(info):
+    info = info.astype(F32)
+    both = jnp.concatenate([info[..., 3:4], info[..., 4:5]], axis=-2)
+    return both.reshape(-1, 1)
 
 
 def fetch_kernel(first_ref, info_ref, table_ref, out_ref):
     groups, per, padded = out_ref.shape
     columns, vocab = table_ref.shape
-    info = info_ref[...].astype(F32)[:, :per]
+    info = info_ref[...].astype(F32)
     ids = info[:, :, 0:1] * 4096.0 + info[:, :, 1:2] * 64.0 + info[:, :, 2:3]
     ids = ids.astype(jnp.int32).reshape(groups * per, 1) - first_ref[0]
     place = lax.broadcasted_iota(jnp.int32, (groups * per, vocab), 1)
@@ -59,24 +76,38 @@
     out_ref[...] = found.astype(BF16).reshape(groups, per, padded)
 
 
-def teacher_kernel(side_ref, rows_ref, info_ref, wl_ref, ww_ref, *rest):
+def teacher_kernel(side_ref, rows_ref, wl_ref, ww_ref, *rest):
     out_ref = rest[-1]
-    places, _, count, width = rows_ref.shape
+    places = rows_ref.shape[0]
+    width = wl_ref.shape[2]
+    count = out_ref.shape[1]
+    steps = count // 2
     half = wl_ref.shape[1]
     wide = ww_ref.shape[1]
     padded = -(-wide // HD) * HD
-    rows = rows_ref[...].reshape(places * count, width)
-    info = info_ref[...].astype(F32).reshape(places * count, HD)
-    first = info[:, 3:4] == 0.0
+    rows = jnp.concatenate(
+        [
+            rows_ref[:, 0, :, k * steps : (k + 1) * steps].reshape(places * count, HD)
+            for k in range(width // HD)
+        ],
+        axis=1,
+    )
+    first = owners(rows_ref[:, 0, :, width // HD * steps :]) == 0.0
+    cut = padded - HD
     for k in range(2):
         one = nt_dot(rows, wl_ref[k])
         two = nt_dot(rows, ww_ref[k])
         one = jnp.concatenate([one, jnp.zeros((places * count, padded - half), F32)], axis=1)
         two = jnp.concatenate([two, jnp.zeros((places * count, padded - wide), F32)], axis=1)
         both = jnp.where(first, one, two).reshape(places, count, padded)
+        head = pl.ds(k * cut, cut)
+        tail = pl.ds(2 * cut + k * HD, HD)
+        main, edge = both[:, :, :cut], both[:, :, cut:]
         if len(rest) > 1:
-            both = both + rest[0][:, :, k * padded : (k + 1) * padded].astype(F32)
-        out_ref[:, :, k * padded : (k + 1) * padded] = both.astype(BF16)
+            main = main + rest[0][:, :, head].astype(F32)
+            edge = edge + rest[0][:, :, tail].astype(F32)
+        out_ref[:, :, head] = main.astype(BF16)
+        out_ref[:, :, tail] = edge.astype(BF16)
 
 
 def student_kernel(side_ref, found_ref, gain_ref, wq_ref, wkv_ref, own_ref, other_ref, query_ref):
@@ -92,10 +123,20 @@
         for p in range(places):
             head = p * KVH // places
             start = pl.multiple_of((2 * p + side) * HD, HD)
-            out_ref[p, :per] = query_ref[:, pl.ds(start, HD)]
-            out_ref[p, per : 2 * per] = pair[:, head * HD : (head + 1) * HD]
-            out_ref[p, 2 * per : 3 * per] = pair[:, (KVH + head) * HD : (KVH + head + 1) * HD]
-            out_ref[p, 3 * per :] = squares
+            own = [
+                query_ref[:, pl.ds(start, HD)],
+                pair[:, head * HD : (head + 1) * HD],
+                pair[:, (KVH + head) * HD : (KVH + head + 1) * HD],
+            ]
+            upper = jnp.concatenate(own, axis=0)[:, : 2 * SPARE]
+            lower = jnp.concatenate([part[:, 2 * SPARE :] for part in own], axis=1)
+            fill = jnp.concatenate([upper, lower], axis=0)
+            pad = jnp.zeros((4 * per, HD - SPARE), F32)
+            sums = jnp.concatenate([squares] * 4, axis=0)
+            lane = lax.broadcasted_iota(jnp.int32, (4 * per, HD), 1)
+            left = jnp.concatenate([pad, fill[:, :SPARE]], axis=1)
+            out_ref[p, :, :HD] = jnp.where(lane == HD - SPARE - 1, sums, left)
+            out_ref[p, :, HD:] = jnp.concatenate([pad, fill[:, SPARE:]], axis=1)
 
 
 def last_kernel(
@@ -103,19 +144,33 @@
 ):
     half = llama_ref.shape[1]
     wide = qwen_ref.shape[1]
-    padded = (parts_ref.shape[2] - HD) // 2
+    cut = parts_ref.shape[2] // 2 - HD
     total = jnp.sum(parts_ref[...].astype(F32), axis=0)
-    gate = total[:, :padded]
-    hidden = gate / (1.0 + jnp.exp(-gate)) * total[:, padded : 2 * padded]
-    first = info_ref[0].astype(F32)[:, 3:4] == 0.0
+    gate = jnp.concatenate([total[:, :cut], total[:, 2 * cut : 2 * cut + HD]], axis=1)
+    up = jnp.concatenate([total[:, cut : 2 * cut], total[:, 2 * cut + HD :]], axis=1)
+    gate, up = gate[:, :wide], up[:, :wide]
+    hidden = gate / (1.0 + jnp.exp(-gate)) * up
+    first = owners(info_ref[0]) == 0.0
     llama_ref[...] = jnp.where(first, hidden, 0.0)[:, :half].astype(BF16)
     qwen_ref[...] = jnp.where(first, 0.0, hidden)[:, :wide].astype(BF16)
 
     rollouts, _, slots, _ = keys_ref.shape
     per = parts_ref.shape[1] // 4
     steps = per // rollouts
-    student = total[:, 2 * padded :]
-    inverse = lax.rsqrt(student[3 * per :] / DS + EPS)
+    keep = HD - SPARE
+    left = total[:, 2 * cut : 2 * cut + HD]
+    fill = jnp.concatenate([left[:, keep:], total[:, 2 * cut + HD + keep :]], axis=1)
+    rest = HD - 2 * SPARE
+    student = jnp.concatenate(
+        [
+            jnp.concatenate(
+                [fill[k * per : (k + 1) * per], fill[3 * per :, k * rest : (k + 1) * rest]], axis=1
+            )
+            for k in range(3)
+        ],
+        axis=0,
+    )
+    inverse = lax.rsqrt(left[:per, keep - 1 : keep] / DS + EPS)
     query = (student[:per] * inverse).astype(BF16)
     key = (student[per : 2 * per] * inverse).astype(BF16)
     value = (student[2 * per : 3 * per] * inverse).astype(BF16)
@@ -198,7 +253,8 @@
     padded = -(-columns // HD) * HD
     half_pad = -(-w_qwen.shape[2] // HD) * HD
     shape = jax.ShapeDtypeStruct
-    block = width // HD
+    lines_held = width // HD * count + per
+    block = width // HD * count // per
 
     first = (lax.axis_index("dp") * vocab).reshape(1)
     core = (tensor_index & 1).reshape(1)
@@ -210,7 +266,7 @@
         [far(tokens), far(rollout_len), far(teacher_of)],
         [far(teacher_rows)],
         [whole_spec(teacher_rows)],
-        [shape((groups, count, width + HD), BF16)],
+        [shape((groups, lines_held, HD), BF16)],
     )
     held, first, core, other, place = lax.optimization_barrier((held, first, core, other, place))
     held = lax.all_to_all(held, "dp", 0, 0, tiled=True)
@@ -223,37 +279,33 @@
         fetch_kernel,
         [first],
         [near(held), near(table)],
-        [
-            pl.BlockSpec((groups, count, HD), lambda i, s: (0, 0, block)),
-            whole_spec(table),
-        ],
+        [pl.BlockSpec((groups, per, HD), lambda i, s: (0, block, 0)), whole_spec(table)],
         [shape((groups, per, padded), BF16)],
     )
+    found, w_qwen = lax.optimization_barrier((found, w_qwen))
     found = lax.all_to_all(found, "dp", 0, 0, tiled=True)
 
-    by_place = near(held.reshape(places, 2, rows_here, width + HD))
+    by_place = near(held.reshape(places, 2, 2, lines_held, HD))
     first_w = near(jnp.transpose(w_llama, (1, 2, 0)))
     second_w = near(jnp.transpose(w_qwen, (1, 2, 0)))
 
-    def teacher(side, extra, width_out):
-        return call(
-            teacher_kernel,
-            [side],
-            [by_place, by_place, first_w, second_w, *extra],
-            [
-                pl.BlockSpec((places, 1, rows_here, width), lambda i, s: (0, s[0], 0, 0)),
-                pl.BlockSpec((places, 1, rows_here, HD), lambda i, s: (0, s[0], 0, block)),
-                whole_spec(first_w),
-                whole_spec(second_w),
-                *[whole_spec(a) for a in extra],
-            ],
-            [shape((places, rows_here, width_out), BF16)],
-        )[0]
-
+    teacher_specs = [
+        pl.BlockSpec((places, 1, 2, lines_held, HD), lambda i, s: (0, s[0], 0, 0, 0)),
+        whole_spec(first_w),
+        whole_spec(second_w),
+    ]
+    teacher_args = [by_place, first_w, second_w]
+    teacher_out = shape((places, rows_here, 2 * half_pad), BF16)
     pairs = [(i, i ^ 1) for i in range(targets)]
-    theirs = teacher(other, [], 2 * half_pad)
+    (theirs,) = call(teacher_kernel, [other], teacher_args, teacher_specs, [teacher_out])
     theirs = lax.ppermute(theirs, "tensor", pairs)
-    joined = teacher(core, [near(theirs)], 2 * half_pad + HD)
+    (joined,) = call(
+        teacher_kernel,
+        [core],
+        teacher_args + [near(theirs)],
+        teacher_specs + [whole_spec(theirs)],
+        [teacher_out],
+    )
 
     gain = norm_gain
     found, joined, gain = lax.optimization_barrier((found, joined, gain))
@@ -263,22 +315,24 @@
             num_scalar_prefetch=1,
             grid=(1,),
             in_specs=[whole_spec(a) for a in (found, gain, w_query, w_key_value)],
-            out_specs=[pl.BlockSpec((places, 4 * per, HD), lambda *_: (0, 0, 0))] * 2,
+            out_specs=[pl.BlockSpec((places, 4 * per, 2 * HD), lambda *_: (0, 0, 0))] * 2,
             scratch_shapes=[pltpu.VMEM((per, w_query.shape[1]), F32)],
         ),
-        out_shape=[pltpu.VMEM((places, 4 * per, HD), F32)] * 2,
+        out_shape=[pltpu.VMEM((places, 4 * per, 2 * HD), F32)] * 2,
         name="student",
         compiler_params=pltpu.CompilerParams(vmem_limit_bytes=VMEM_LIMIT),
-    )(core, near(found), gain, far(w_query), far(w_key_value))
+    )(core, near(found), gain, near(w_query), near(w_key_value))
     theirs = lax.ppermute(theirs, "tensor", pairs)
-    joined = lax.dynamic_update_slice(joined, (ours + theirs).astype(BF16), (0, 0, 2 * half_pad))
+    cut = 2 * (half_pad - HD)
+    tails = joined[:, :, cut:].astype(F32) + (ours + theirs)
+    joined = lax.dynamic_update_slice(joined, tails.astype(BF16), (0, 0, cut))
 
     lines = [[2 * p + c for p in range(places)] for c in range(2)]
     joined, place, cache_len = lax.optimization_barrier((joined, place, cache_len))
     parts = lax.all_to_all(joined, "tensor", 0, 0, axis_index_groups=lines, tiled=True)
     parts, place, cache_len = lax.optimization_barrier((parts, place, cache_len))
 
-    by_target = held.reshape(targets, rows_here, width + HD)
+    by_target = held.reshape(targets, 2, lines_held, HD)
     slots = cache_keys.shape[2]
     cache_spec = pl.BlockSpec((rollouts, 1, slots, HD), lambda i, s, _: (0, s[1], 0, 0))
     return tuple(call(
@@ -287,7 +341,7 @@
         [near(parts), near(by_target), cache_keys, cache_values],
         [
             whole_spec(parts),
-            pl.BlockSpec((1, rows_here, HD), lambda i, s, _: (s[0], 0, block)),
+            pl.BlockSpec((1, 2, per, HD), lambda i, s, _: (s[0], 0, block, 0)),
             cache_spec,
             cache_spec,
         ],

time: 91 us -> 88.7 us (0.975)
  blocking collectives: 57.2 us -> 54.4 us
  waiting for transfers between devices: 8.29 us -> 9.24 us
    all_to_all x1, blocking collectives: 25 us -> 23.3 us  [shards(): lax.all_to_all(joined, 'tensor', 0, 0, axis_index_groups=lines, tiled=True)]
    all_to_all x1, blocking collectives: 32.2 us -> 31.1 us  [shards(): held = lax.all_to_all(held, 'dp', 0, 0, tiled=True)]
    pallas_call x1, Pallas kernels: 1.6 us -> 0.49 us  [shards(): pl.pallas_call(student_kernel, grid_spec=pltpu.PrefetchScalarGridSpec(num...]
where the time goes in v3:
time: 88.7 us; the launch traced here: 88.2 us
  blocking collectives  54.4 us (61%)
  starting transfers between devices  12.3 us (14%)
  waiting for transfers between devices  9.24 us (10%)
  Pallas kernels  7.94 us (9%)
  local copies, waits for them, and re-layouts  3.41 us (4%)
    all_to_all x1, blocking collectives, shards(): held = lax.all_to_all(held, 'dp', 0, 0, tiled=True)  31.1 us
    all_to_all x1, blocking collectives, shards(): lax.all_to_all(joined, 'tensor', 0, 0, axis_index_groups=lines, tiled=True)  23.3 us
    all_to_all x1, waiting for transfers between devices, shards(): found = lax.all_to_all(found, 'dp', 0, 0, tiled=True)  8.09 us
    ppermute x2, starting transfers between devices, shards(): theirs = lax.ppermute(theirs, 'tensor', pairs)  7.77 us
    pallas_call x5, Pallas kernels, call(): pl.pallas_call(kernel, grid_spec=pltpu.PrefetchScalarGridSpec(num_scalar_...  7.45 us
    all_to_all x1, starting transfers between devices, shards(): found = lax.all_to_all(found, 'dp', 0, 0, tiled=True)  4.54 us
    unnamed x18, local copies, waits for them, and re-layouts  3.26 us
  transfers between devices with their start and end apart: 3, of which 2 were waited for; matrix products, arithmetic and copies ran while one was open for 0% of the time, Pallas kernels for 2%

profile of v3, /device:TPU:1, one launch (start us, length us, event | category | flops | bytes accessed | tf_op | source)
XLA Modules:
  0.0 88.2 jit_solution(5663353358642616545)
XLA Ops:
  0.6 0.0 copy-start.1
  0.6 0.1 pad_add_fusion.place_ref
  0.7 1.6 %shard_map.148 = bf16[32,72,128]{2,1,0:T(8,128)(2,1)S(1)} custom-call(s32[2,4]{1,0:T(2,128)} %tokens_ref.1, s32[1,4]{1,0:T(1,128)} %lens_ref.1, s32[1,4]{1,0:T(1,128)} %kinds_ref.1, bf16[16,512]{1,0:T(8,128)(2,1)} %rows_ref.1), custom_call_target="tpu_custom_call" | custom-call | tf_op jit(solution)/shard_map/pallas_call | solution.py:216
  2.3 31.1 %all_to_all.15.info_ref = bf16[32,72,128]{2,1,0:T(8,128)(2,1)S(1)} all-to-all(bf16[32,72,128]{2,1,0:T(8,128)(2,1)S(1)} %shard_map.148), channel_id=1, replica_groups=mesh['dp'=32,'tensor'=16] {'dp'}, dimensions={0} | all-to-all | bytes 1179648 | tf_op jit(solution)/shard_map/all_to_all | solution.py:272
  33.4 0.0 copy-start.8
  33.4 0.0 copy-done.1
  33.4 1.3 %shard_map.149 = bf16[32,8,256]{2,1,0:T(8,128)(2,1)} custom-call(s32[1]{0:T(128)} %bitcast.first_ref, bf16[32,72,128]{2,1,0:T(8,128)(2,1)S(1)} %all_to_all.15.info_ref, bf16[224,2432]{1,0:T(8,128)(2,1)S(1)} %bitcast.18), custom_call_target="tpu_custom_call" | custom-call | tf_op jit(solution)/shard_map/pallas_call | solution.py:216
  34.7 0.0 copy-done.8
  34.7 0.0 copy-start
  34.7 0.1 copy.18
  34.9 1.0 %copy-done = bf16[512,2,448]{0,2,1:T(8,128)(2,1)S(1)} copy-done((bf16[512,2,448]{0,2,1:T(8,128)(2,1)S(1)}, bf16[512,2,448]{0,2,1:T(8,128)(2,1)}, u32[]{:S(2)}) %copy-start) | copy-done | bytes 917528
  35.9 0.7 shard_map.150
  36.6 4.3 %collective-permute-start = (bf16[8,32,1024]{2,1,0:T(8,128)(2,1)S(1)}, bf16[8,32,1024]{2,1,0:T(8,128)(2,1)}, u32[]{:S(2)}, u32[]{:S(2)}) collective-permute-start(bf16[8,32,1024]{2,1,0:T(8,128)(2,1)S(1)} %shard_map.150), channel_id=1, source_target_pairs={{0,1},{1,0},{2,3},{3,2},{4,5},{5,4},{6,7},{7,6},{8,9},{9,8},{10,11... | collective-permute-start | bytes 1572872 | tf_op jit(solution)/shard_map/ppermute | solution.py:301
  40.9 4.5 %all-to-all-start.1 = ((bf16[32,8,256]{2,1,0:T(8,128)(2,1)}), bf16[32,8,256]{2,1,0:T(8,128)(2,1)S(1)}, u32[]{:S(2)}, u32[]{:S(2)}) async-start(bf16[32,8,256]{2,1,0:T(8,128)(2,1)} %shard_map.149), calls=%async_computation.1 | async-start | bytes 262144 | tf_op jit(solution)/shard_map/all_to_all | solution.py:286
  45.5 0.0 copy-start.6
  45.5 0.0 collective-permute-done.rest_0_
  45.5 1.8 %shard_map.151 = bf16[8,32,1024]{2,1,0:T(8,128)(2,1)S(1)} custom-call(s32[1]{0:T(128)} %bitcast.1.side_ref, bf16[8,2,2,72,128]{4,3,2,1,0:T(8,128)(2,1)S(1)} %bitcast.12, bf16[2,448,512]{2,1,0:T(8,128)(2,1)S(1)} %bitcast.17, bf16[2,462,512]{2,1,0:T(8,128)(2,1)S(1)} %bitcast.15, bf16[8,32,1024]{2,1,0:T(8,128)(2,1)} %collective-permute-done.rest_0_), custom_call_target="tpu_custom_call" | custom-call | tf_op jit(solution)/shard_map/pallas_call | solution.py:216
  47.3 8.1 %all-to-all-done.1.found_ref = bf16[32,8,256]{2,1,0:T(8,128)(2,1)S(1)} async-done(((bf16[32,8,256]{2,1,0:T(8,128)(2,1)}), bf16[32,8,256]{2,1,0:T(8,128)(2,1)S(1)}, u32[]{:S(2)}, u32[]{:S(2)}) %all-to-all-start.1) | async-done | bytes 131104 | tf_op jit(solution)/shard_map/all_to_all | solution.py:286
  55.4 0.0 copy-done.6
  55.4 0.0 copy-start.2
  55.4 1.2 %copy-done.2 = bf16[224,2048]{1,0:T(8,128)(2,1)S(1)} copy-done((bf16[224,2048]{1,0:T(8,128)(2,1)S(1)}, bf16[224,2048]{1,0:T(8,128)(2,1)}, u32[]{:S(2)}) %copy-start.2) | copy-done | bytes 917528
  56.6 0.0 copy-start.3
  56.6 1.0 %copy-done.3 = bf16[224,1024]{1,0:T(8,128)(2,1)S(1)} copy-done((bf16[224,1024]{1,0:T(8,128)(2,1)S(1)}, bf16[224,1024]{1,0:T(8,128)(2,1)}, u32[]{:S(2)}) %copy-start.3) | copy-done | bytes 458776
  57.6 0.5 student.1
  58.1 0.0 copy-start.4
  58.1 0.0 copy-start.5
  58.1 0.0 copy-start.7
  58.2 3.5 %collective-permute-start.1 = (f32[8,32,256]{2,1,0:T(8,128)S(1)}, f32[8,32,256]{2,1,0:T(8,128)S(1)}, u32[]{:S(2)}, u32[]{:S(2)}) collective-permute-start(f32[8,32,256]{2,1,0:T(8,128)S(1)} %get-tuple-element.38), channel_id=1, source_target_pairs={{0,1},{1,0},{2,3},{3,2},{4,5},{5,4},{6,7},{7,6},{8,9},{9,8},{10,11... | collective-permute-start | bytes 786440 | tf_op jit(solution)/shard_map/ppermute | solution.py:325
  61.6 1.1 %collective-permute-done.1 = f32[8,32,256]{2,1,0:T(8,128)S(1)} collective-permute-done((f32[8,32,256]{2,1,0:T(8,128)S(1)}, f32[8,32,256]{2,1,0:T(8,128)S(1)}, u32[]{:S(2)}, u32[]{:S(2)}) %collective-permute-start.1) | collective-permute-done | bytes 262176 | tf_op jit(solution)/shard_map/ppermute | solution.py:325
  62.8 23.3 %all_to_all.16.parts_ref = bf16[8,32,1024]{2,1,0:T(8,128)(2,1)S(1)} all-to-all(bf16[8,32,1024]{2,1,0:T(8,128)(2,1)S(1)} %fusion), channel_id=1, replica_groups={{0,2,4,6,8,10,12,14},{1,3,5,7,9,11,13,15},{16,18,20,22,24,26,28,30},{17..., dimensions={0} | all-to-all | bytes 1048576 | tf_op jit(solution)/shard_map/all_to_all | solution.py:332
  86.2 0.0 copy-done.4
  86.2 0.0 copy-done.5
  86.2 0.0 copy-done.7
  86.2 2.0 %shard_map.152 = (bf16[2,4,128]{2,1,0:T(4,128)(2,1)}, bf16[32,448]{1,0:T(8,128)(2,1)}, bf16[32,462]{1,0:T(8,128)(2,1)}) custom-call(s32[2]{0:T(128)S(1)} %pad_add_fusion.place_ref, s32[2]{0:T(128)S(1)} %copy-done.7, bf16[8,32,1024]{2,1,0:T(8,128)(2,1)S(1)} %all_to_all.16.parts_ref, bf16[16,2,72,128]{3,2,1,0:T(8,128)(2,1)S(1)} %bitcast.13, ...), custom_call_target="tpu_custom_call" | custom-call | tf_op jit(solution)/shard_map/pallas_call | solution.py:216
  (1 shorter events, 0.0 us)
Async XLA Ops:
  0.6 32.8 %copy-start.1 = (bf16[2432,224]{0,1:T(8,128)(2,1)S(1)}, bf16[2432,224]{0,1:T(8,128)(2,1)}, u32[]{:S(2)}) copy-start(bf16[2432,224]{0,1:T(8,128)(2,1)} %param.14) | copy-start | bytes 3268612
  33.4 1.3 %copy-start.8 = (bf16[512,2,462]{0,1,2:T(2,128)(2,1)S(1)}, bf16[512,2,462]{0,1,2:T(2,128)(2,1)}, u32[]{:S(2)}) copy-start(bf16[512,2,462]{0,1,2:T(2,128)(2,1)} %param.23) | copy-start | bytes 2838532
  34.7 1.2 %copy-start = (bf16[512,2,448]{0,2,1:T(8,128)(2,1)S(1)}, bf16[512,2,448]{0,2,1:T(8,128)(2,1)}, u32[]{:S(2)}) copy-start(bf16[512,2,448]{0,2,1:T(8,128)(2,1)} %param.22) | copy-start | bytes 2752516
  36.6 8.9 %collective-permute-start = (bf16[8,32,1024]{2,1,0:T(8,128)(2,1)S(1)}, bf16[8,32,1024]{2,1,0:T(8,128)(2,1)}, u32[]{:S(2)}, u32[]{:S(2)}) collective-permute-start(bf16[8,32,1024]{2,1,0:T(8,128)(2,1)S(1)} %shard_map.150), channel_id=1, source_target_pairs={{0,1},{1,0},{2,3},{3,2},{4,5},{5,4},{6,7},{7,6},{8,9},{9,8},{10,11... | collective-permute-start | bytes 1572872 | tf_op jit(solution)/shard_map/ppermute | solution.py:301
  40.9 14.5 %all-to-all-start.1 = ((bf16[32,8,256]{2,1,0:T(8,128)(2,1)}), bf16[32,8,256]{2,1,0:T(8,128)(2,1)S(1)}, u32[]{:S(2)}, u32[]{:S(2)}) async-start(bf16[32,8,256]{2,1,0:T(8,128)(2,1)} %shard_map.149), calls=%async_computation.1 | async-start | bytes 262144 | tf_op jit(solution)/shard_map/all_to_all | solution.py:286
  45.5 9.9 %copy-start.6 = (bf16[224]{0:T(256)(128)(2,1)S(1)}, bf16[224]{0:T(256)(128)(2,1)}, u32[]{:S(2)}) copy-start(bf16[224]{0:T(256)(128)(2,1)} %gain_ref) | copy-start | bytes 1348
  55.4 1.2 %copy-start.2 = (bf16[224,2048]{1,0:T(8,128)(2,1)S(1)}, bf16[224,2048]{1,0:T(8,128)(2,1)}, u32[]{:S(2)}) copy-start(bf16[224,2048]{1,0:T(8,128)(2,1)} %wq_ref.1) | copy-start | bytes 2752516
  56.6 1.0 %copy-start.3 = (bf16[224,1024]{1,0:T(8,128)(2,1)S(1)}, bf16[224,1024]{1,0:T(8,128)(2,1)}, u32[]{:S(2)}) copy-start(bf16[224,1024]{1,0:T(8,128)(2,1)} %wkv_ref.1) | copy-start | bytes 1376260
  58.1 28.1 %copy-start.4 = (bf16[2,4,64,128]{3,2,1,0:T(8,128)(2,1)S(1)}, bf16[2,4,64,128]{3,2,1,0:T(8,128)(2,1)}, u32[]{:S(2)}) copy-start(bf16[2,4,64,128]{3,2,1,0:T(8,128)(2,1)} %keys_ref.1) | copy-start | bytes 393220
  58.1 28.0 %copy-start.5 = (bf16[2,4,64,128]{3,2,1,0:T(8,128)(2,1)S(1)}, bf16[2,4,64,128]{3,2,1,0:T(8,128)(2,1)}, u32[]{:S(2)}) copy-start(bf16[2,4,64,128]{3,2,1,0:T(8,128)(2,1)} %values_ref.1) | copy-start | bytes 393220
  58.1 28.0 %copy-start.7 = (s32[2]{0:T(128)S(1)}, s32[2]{0:T(128)}, u32[]{:S(2)}) copy-start(s32[2]{0:T(128)} %sizes_ref) | copy-start | bytes 28
  58.2 4.6 %collective-permute-start.1 = (f32[8,32,256]{2,1,0:T(8,128)S(1)}, f32[8,32,256]{2,1,0:T(8,128)S(1)}, u32[]{:S(2)}, u32[]{:S(2)}) collective-permute-start(f32[8,32,256]{2,1,0:T(8,128)S(1)} %get-tuple-element.38), channel_id=1, source_target_pairs={{0,1},{1,0},{2,3},{3,2},{4,5},{5,4},{6,7},{7,6},{8,9},{9,8},{10,11... | collective-permute-start | bytes 786440 | tf_op jit(solution)/shard_map/ppermute | solution.py:325

commit v4 on v3

--- a/solution.py
+++ b/solution.py
@@ -14,7 +14,7 @@
 F32 = jnp.float32
 BF16 = jnp.bfloat16
 SPARE = 48
-VMEM_LIMIT = 28 * 2**20
+VMEM_LIMIT = 16 * 2**20
 
 
 def nt_dot(a, b):
@@ -31,22 +31,21 @@
     sub = lax.broadcasted_iota(jnp.int32, (per, HD), 0)
     info = jnp.zeros((per, HD), jnp.int32)
     for s in range(tokens_ref.shape[0] * steps):
-        token = tokens_ref[s // steps, s % steps]
+        token = tokens_ref[s // steps : s // steps + 1, s % steps : s % steps + 1]
         digits = jnp.where(
             lane == 0, token >> 12, jnp.where(lane == 1, (token >> 6) & 63, token & 63)
         )
         info = jnp.where(jnp.logical_and(sub == s, lane < 3), digits, info)
-    one = lens_ref[0, 0]
-    two = one + lens_ref[0, 1]
-    three = two + lens_ref[0, 2]
+    kinds = [kinds_ref[:, k : k + 1] for k in range(4)]
+    one = lens_ref[:, 0:1]
+    two = one + lens_ref[:, 1:2]
+    three = two + lens_ref[:, 2:3]
     for half in range(count // per):
         row = sub + half * per
         owner = jnp.where(
             row < one,
-            kinds_ref[0, 0],
-            jnp.where(
-                row < two, kinds_ref[0, 1], jnp.where(row < three, kinds_ref[0, 2], kinds_ref[0, 3])
-            ),
+            kinds[0],
+            jnp.where(row < two, kinds[1], jnp.where(row < three, kinds[2], kinds[3])),
         )
         info = jnp.where(lane == 3 + half, owner, info)
     rows = rows_ref[...]
@@ -263,9 +262,9 @@
 
     (held,) = call(
         pack_kernel,
-        [far(tokens), far(rollout_len), far(teacher_of)],
-        [far(teacher_rows)],
-        [whole_spec(teacher_rows)],
+        [],
+        [far(a) for a in (tokens, rollout_len, teacher_of, teacher_rows)],
+        [whole_spec(a) for a in (tokens, rollout_len, teacher_of, teacher_rows)],
         [shape((groups, lines_held, HD), BF16)],
     )
     held, first, core, other, place = lax.optimization_barrier((held, first, core, other, place))
@@ -306,10 +305,8 @@
         teacher_specs + [whole_spec(theirs)],
         [teacher_out],
     )
-
-    gain = norm_gain
-    found, joined, gain = lax.optimization_barrier((found, joined, gain))
-    ours, theirs = pl.pallas_call(
+    found, joined, gain = lax.optimization_barrier((found, joined, norm_gain))
+    ours, swapped = pl.pallas_call(
         student_kernel,
         grid_spec=pltpu.PrefetchScalarGridSpec(
             num_scalar_prefetch=1,
@@ -322,9 +319,9 @@
         name="student",
         compiler_params=pltpu.CompilerParams(vmem_limit_bytes=VMEM_LIMIT),
     )(core, near(found), gain, near(w_query), near(w_key_value))
-    theirs = lax.ppermute(theirs, "tensor", pairs)
+    swapped = lax.ppermute(swapped, "tensor", pairs)
     cut = 2 * (half_pad - HD)
-    tails = joined[:, :, cut:].astype(F32) + (ours + theirs)
+    tails = joined[:, :, cut:].astype(F32) + (ours + swapped)
     joined = lax.dynamic_update_slice(joined, tails.astype(BF16), (0, 0, cut))
 
     lines = [[2 * p + c for p in range(places)] for c in range(2)]

time: 88.7 us -> 88 us (level)
    ppermute x0 -> x1, starting transfers between devices: none -> 3.47 us  [shards(): swapped = lax.ppermute(swapped, 'tensor', pairs)]
    ppermute x2 -> x1, starting transfers between devices: 7.77 us -> 4.3 us  [shards(): theirs = lax.ppermute(theirs, 'tensor', pairs)]
    ppermute x2 -> x1, waiting for transfers between devices: 1.14 us -> 0.01 us  [shards(): theirs = lax.ppermute(theirs, 'tensor', pairs)]
    ppermute x0 -> x1, waiting for transfers between devices: none -> 1.14 us  [shards(): swapped = lax.ppermute(swapped, 'tensor', pairs)]
where the time goes in v4:
time: 88 us; the launch traced here: 87.6 us
  blocking collectives  54.4 us (62%)
  starting transfers between devices  12.3 us (14%)
  waiting for transfers between devices  9.23 us (10%)
  Pallas kernels  7.32 us (8%)
  local copies, waits for them, and re-layouts  3.41 us (4%)
    all_to_all x1, blocking collectives, shards(): held = lax.all_to_all(held, 'dp', 0, 0, tiled=True)  31.1 us
    all_to_all x1, blocking collectives, shards(): lax.all_to_all(joined, 'tensor', 0, 0, axis_index_groups=lines, tiled=True)  23.3 us
    all_to_all x1, waiting for transfers between devices, shards(): found = lax.all_to_all(found, 'dp', 0, 0, tiled=True)  8.09 us
    pallas_call x5, Pallas kernels, call(): pl.pallas_call(kernel, grid_spec=pltpu.PrefetchScalarGridSpec(num_scalar_...  6.82 us
    all_to_all x1, starting transfers between devices, shards(): found = lax.all_to_all(found, 'dp', 0, 0, tiled=True)  4.54 us
    ppermute x1, starting transfers between devices, shards(): theirs = lax.ppermute(theirs, 'tensor', pairs)  4.3 us
    ppermute x1, starting transfers between devices, shards(): swapped = lax.ppermute(swapped, 'tensor', pairs)  3.47 us
    unnamed x18, local copies, waits for them, and re-layouts  3.26 us
  transfers between devices with their start and end apart: 3, of which 2 were waited for; matrix products, arithmetic and copies ran while one was open for 0% of the time, Pallas kernels for 2%

profile of v4, /device:TPU:1, one launch (start us, length us, event | category | flops | bytes accessed | tf_op | source)
XLA Modules:
  0.0 87.6 jit_solution(10100835791074311132)
XLA Ops:
  0.6 0.0 copy-start.1
  0.6 0.1 pad_add_fusion.place_ref
  0.7 1.0 %shard_map.148 = bf16[32,72,128]{2,1,0:T(8,128)(2,1)S(1)} custom-call(s32[2,4]{1,0:T(2,128)} %tokens_ref.1, s32[1,4]{1,0:T(1,128)} %lens_ref.1, s32[1,4]{1,0:T(1,128)} %kinds_ref.1, bf16[16,512]{1,0:T(8,128)(2,1)} %rows_ref.1), custom_call_target="tpu_custom_call" | custom-call | tf_op jit(solution)/shard_map/pallas_call | solution.py:215
  1.7 31.1 %all_to_all.15.info_ref = bf16[32,72,128]{2,1,0:T(8,128)(2,1)S(1)} all-to-all(bf16[32,72,128]{2,1,0:T(8,128)(2,1)S(1)} %shard_map.148), channel_id=1, replica_groups=mesh['dp'=32,'tensor'=16] {'dp'}, dimensions={0} | all-to-all | bytes 1179648 | tf_op jit(solution)/shard_map/all_to_all | solution.py:271
  32.8 0.0 copy-start.8
  32.8 0.0 copy-done.1
  32.8 1.3 %shard_map.149 = bf16[32,8,256]{2,1,0:T(8,128)(2,1)} custom-call(s32[1]{0:T(128)} %bitcast.first_ref, bf16[32,72,128]{2,1,0:T(8,128)(2,1)S(1)} %all_to_all.15.info_ref, bf16[224,2432]{1,0:T(8,128)(2,1)S(1)} %bitcast.18), custom_call_target="tpu_custom_call" | custom-call | tf_op jit(solution)/shard_map/pallas_call | solution.py:215
  34.1 0.0 copy-done.8
  34.1 0.0 copy-start
  34.1 0.1 copy.18
  34.3 1.0 %copy-done = bf16[512,2,448]{0,2,1:T(8,128)(2,1)S(1)} copy-done((bf16[512,2,448]{0,2,1:T(8,128)(2,1)S(1)}, bf16[512,2,448]{0,2,1:T(8,128)(2,1)}, u32[]{:S(2)}) %copy-start) | copy-done | bytes 917528
  35.3 0.7 shard_map.150
  36.0 4.3 %collective-permute-start = (bf16[8,32,1024]{2,1,0:T(8,128)(2,1)S(1)}, bf16[8,32,1024]{2,1,0:T(8,128)(2,1)}, u32[]{:S(2)}, u32[]{:S(2)}) collective-permute-start(bf16[8,32,1024]{2,1,0:T(8,128)(2,1)S(1)} %shard_map.150), channel_id=1, source_target_pairs={{0,1},{1,0},{2,3},{3,2},{4,5},{5,4},{6,7},{7,6},{8,9},{9,8},{10,11... | collective-permute-start | bytes 1572872 | tf_op jit(solution)/shard_map/ppermute | solution.py:300
  40.3 4.5 %all-to-all-start.1 = ((bf16[32,8,256]{2,1,0:T(8,128)(2,1)}), bf16[32,8,256]{2,1,0:T(8,128)(2,1)S(1)}, u32[]{:S(2)}, u32[]{:S(2)}) async-start(bf16[32,8,256]{2,1,0:T(8,128)(2,1)} %shard_map.149), calls=%async_computation.1 | async-start | bytes 262144 | tf_op jit(solution)/shard_map/all_to_all | solution.py:285
  44.9 0.0 copy-start.6
  44.9 0.0 collective-permute-done.rest_0_
  44.9 1.8 %shard_map.151 = bf16[8,32,1024]{2,1,0:T(8,128)(2,1)S(1)} custom-call(s32[1]{0:T(128)} %bitcast.1.side_ref, bf16[8,2,2,72,128]{4,3,2,1,0:T(8,128)(2,1)S(1)} %bitcast.12, bf16[2,448,512]{2,1,0:T(8,128)(2,1)S(1)} %bitcast.17, bf16[2,462,512]{2,1,0:T(8,128)(2,1)S(1)} %bitcast.15, bf16[8,32,1024]{2,1,0:T(8,128)(2,1)} %collective-permute-done.rest_0_), custom_call_target="tpu_custom_call" | custom-call | tf_op jit(solution)/shard_map/pallas_call | solution.py:215
  46.7 8.1 %all-to-all-done.1.found_ref = bf16[32,8,256]{2,1,0:T(8,128)(2,1)S(1)} async-done(((bf16[32,8,256]{2,1,0:T(8,128)(2,1)}), bf16[32,8,256]{2,1,0:T(8,128)(2,1)S(1)}, u32[]{:S(2)}, u32[]{:S(2)}) %all-to-all-start.1) | async-done | bytes 131104 | tf_op jit(solution)/shard_map/all_to_all | solution.py:285
  54.8 0.0 copy-done.6
  54.8 0.0 copy-start.2
  54.8 1.2 %copy-done.2 = bf16[224,2048]{1,0:T(8,128)(2,1)S(1)} copy-done((bf16[224,2048]{1,0:T(8,128)(2,1)S(1)}, bf16[224,2048]{1,0:T(8,128)(2,1)}, u32[]{:S(2)}) %copy-start.2) | copy-done | bytes 917528
  56.0 0.0 copy-start.3
  56.0 1.0 %copy-done.3 = bf16[224,1024]{1,0:T(8,128)(2,1)S(1)} copy-done((bf16[224,1024]{1,0:T(8,128)(2,1)S(1)}, bf16[224,1024]{1,0:T(8,128)(2,1)}, u32[]{:S(2)}) %copy-start.3) | copy-done | bytes 458776
  57.0 0.5 student.1
  57.5 0.0 copy-start.4
  57.5 0.0 copy-start.5
  57.5 0.0 copy-start.7
  57.5 3.5 %collective-permute-start.1 = (f32[8,32,256]{2,1,0:T(8,128)S(1)}, f32[8,32,256]{2,1,0:T(8,128)S(1)}, u32[]{:S(2)}, u32[]{:S(2)}) collective-permute-start(f32[8,32,256]{2,1,0:T(8,128)S(1)} %get-tuple-element.38), channel_id=1, source_target_pairs={{0,1},{1,0},{2,3},{3,2},{4,5},{5,4},{6,7},{7,6},{8,9},{9,8},{10,11... | collective-permute-start | bytes 786440 | tf_op jit(solution)/shard_map/ppermute | solution.py:322
  61.0 1.1 %collective-permute-done.1 = f32[8,32,256]{2,1,0:T(8,128)S(1)} collective-permute-done((f32[8,32,256]{2,1,0:T(8,128)S(1)}, f32[8,32,256]{2,1,0:T(8,128)S(1)}, u32[]{:S(2)}, u32[]{:S(2)}) %collective-permute-start.1) | collective-permute-done | bytes 262176 | tf_op jit(solution)/shard_map/ppermute | solution.py:322
  62.2 23.3 %all_to_all.16.parts_ref = bf16[8,32,1024]{2,1,0:T(8,128)(2,1)S(1)} all-to-all(bf16[8,32,1024]{2,1,0:T(8,128)(2,1)S(1)} %fusion), channel_id=1, replica_groups={{0,2,4,6,8,10,12,14},{1,3,5,7,9,11,13,15},{16,18,20,22,24,26,28,30},{17..., dimensions={0} | all-to-all | bytes 1048576 | tf_op jit(solution)/shard_map/all_to_all | solution.py:329
  85.6 0.0 copy-done.4
  85.6 0.0 copy-done.5
  85.6 0.0 copy-done.7
  85.6 2.0 %shard_map.152 = (bf16[2,4,128]{2,1,0:T(4,128)(2,1)}, bf16[32,448]{1,0:T(8,128)(2,1)}, bf16[32,462]{1,0:T(8,128)(2,1)}) custom-call(s32[2]{0:T(128)S(1)} %pad_add_fusion.place_ref, s32[2]{0:T(128)S(1)} %copy-done.7, bf16[8,32,1024]{2,1,0:T(8,128)(2,1)S(1)} %all_to_all.16.parts_ref, bf16[16,2,72,128]{3,2,1,0:T(8,128)(2,1)S(1)} %bitcast.13, ...), custom_call_target="tpu_custom_call" | custom-call | tf_op jit(solution)/shard_map/pallas_call | solution.py:215
  (1 shorter events, 0.0 us)
Async XLA Ops:
  0.6 32.2 %copy-start.1 = (bf16[2432,224]{0,1:T(8,128)(2,1)S(1)}, bf16[2432,224]{0,1:T(8,128)(2,1)}, u32[]{:S(2)}) copy-start(bf16[2432,224]{0,1:T(8,128)(2,1)} %param.14) | copy-start | bytes 3268612
  32.8 1.3 %copy-start.8 = (bf16[512,2,462]{0,1,2:T(2,128)(2,1)S(1)}, bf16[512,2,462]{0,1,2:T(2,128)(2,1)}, u32[]{:S(2)}) copy-start(bf16[512,2,462]{0,1,2:T(2,128)(2,1)} %param.23) | copy-start | bytes 2838532
  34.1 1.2 %copy-start = (bf16[512,2,448]{0,2,1:T(8,128)(2,1)S(1)}, bf16[512,2,448]{0,2,1:T(8,128)(2,1)}, u32[]{:S(2)}) copy-start(bf16[512,2,448]{0,2,1:T(8,128)(2,1)} %param.22) | copy-start | bytes 2752516
  36.0 8.9 %collective-permute-start = (bf16[8,32,1024]{2,1,0:T(8,128)(2,1)S(1)}, bf16[8,32,1024]{2,1,0:T(8,128)(2,1)}, u32[]{:S(2)}, u32[]{:S(2)}) collective-permute-start(bf16[8,32,1024]{2,1,0:T(8,128)(2,1)S(1)} %shard_map.150), channel_id=1, source_target_pairs={{0,1},{1,0},{2,3},{3,2},{4,5},{5,4},{6,7},{7,6},{8,9},{9,8},{10,11... | collective-permute-start | bytes 1572872 | tf_op jit(solution)/shard_map/ppermute | solution.py:300
  40.3 14.5 %all-to-all-start.1 = ((bf16[32,8,256]{2,1,0:T(8,128)(2,1)}), bf16[32,8,256]{2,1,0:T(8,128)(2,1)S(1)}, u32[]{:S(2)}, u32[]{:S(2)}) async-start(bf16[32,8,256]{2,1,0:T(8,128)(2,1)} %shard_map.149), calls=%async_computation.1 | async-start | bytes 262144 | tf_op jit(solution)/shard_map/all_to_all | solution.py:285
  44.9 9.9 %copy-start.6 = (bf16[224]{0:T(256)(128)(2,1)S(1)}, bf16[224]{0:T(256)(128)(2,1)}, u32[]{:S(2)}) copy-start(bf16[224]{0:T(256)(128)(2,1)} %gain_ref) | copy-start | bytes 1348
  54.8 1.2 %copy-start.2 = (bf16[224,2048]{1,0:T(8,128)(2,1)S(1)}, bf16[224,2048]{1,0:T(8,128)(2,1)}, u32[]{:S(2)}) copy-start(bf16[224,2048]{1,0:T(8,128)(2,1)} %wq_ref.1) | copy-start | bytes 2752516
  56.0 1.0 %copy-start.3 = (bf16[224,1024]{1,0:T(8,128)(2,1)S(1)}, bf16[224,1024]{1,0:T(8,128)(2,1)}, u32[]{:S(2)}) copy-start(bf16[224,1024]{1,0:T(8,128)(2,1)} %wkv_ref.1) | copy-start | bytes 1376260
  57.5 28.1 %copy-start.4 = (bf16[2,4,64,128]{3,2,1,0:T(8,128)(2,1)S(1)}, bf16[2,4,64,128]{3,2,1,0:T(8,128)(2,1)}, u32[]{:S(2)}) copy-start(bf16[2,4,64,128]{3,2,1,0:T(8,128)(2,1)} %keys_ref.1) | copy-start | bytes 393220
  57.5 28.0 %copy-start.5 = (bf16[2,4,64,128]{3,2,1,0:T(8,128)(2,1)S(1)}, bf16[2,4,64,128]{3,2,1,0:T(8,128)(2,1)}, u32[]{:S(2)}) copy-start(bf16[2,4,64,128]{3,2,1,0:T(8,128)(2,1)} %values_ref.1) | copy-start | bytes 393220
  57.5 28.0 %copy-start.7 = (s32[2]{0:T(128)S(1)}, s32[2]{0:T(128)}, u32[]{:S(2)}) copy-start(s32[2]{0:T(128)} %sizes_ref) | copy-start | bytes 28
  57.5 4.6 %collective-permute-start.1 = (f32[8,32,256]{2,1,0:T(8,128)S(1)}, f32[8,32,256]{2,1,0:T(8,128)S(1)}, u32[]{:S(2)}, u32[]{:S(2)}) collective-permute-start(f32[8,32,256]{2,1,0:T(8,128)S(1)} %get-tuple-element.38), channel_id=1, source_target_pairs={{0,1},{1,0},{2,3},{3,2},{4,5},{5,4},{6,7},{7,6},{8,9},{9,8},{10,11... | collective-permute-start | bytes 786440 | tf_op jit(solution)/shard_map/ppermute | solution.py:322

commit v5 on v4

--- a/solution.py
+++ b/solution.py
@@ -63,16 +63,15 @@
 
 
 def fetch_kernel(first_ref, info_ref, table_ref, out_ref):
-    groups, per, padded = out_ref.shape
-    columns, vocab = table_ref.shape
+    groups, per, columns = out_ref.shape
+    vocab = table_ref.shape[1]
     info = info_ref[...].astype(F32)
     ids = info[:, :, 0:1] * 4096.0 + info[:, :, 1:2] * 64.0 + info[:, :, 2:3]
     ids = ids.astype(jnp.int32).reshape(groups * per, 1) - first_ref[0]
     place = lax.broadcasted_iota(jnp.int32, (groups * per, vocab), 1)
     hot = jnp.where(ids == place, 1.0, 0.0).astype(BF16)
     found = nt_dot(hot, table_ref[...])
-    found = jnp.concatenate([found, jnp.zeros((groups * per, padded - columns), F32)], axis=1)
-    out_ref[...] = found.astype(BF16).reshape(groups, per, padded)
+    out_ref[...] = found.astype(BF16).reshape(groups, per, columns)
 
 
 def teacher_kernel(side_ref, rows_ref, wl_ref, ww_ref, *rest):
@@ -113,7 +112,7 @@
     places = own_ref.shape[0]
     per = found_ref.shape[1]
     columns = wq_ref.shape[0]
-    x = jnp.sum(found_ref[...].astype(F32), axis=0)[:, :columns]
+    x = jnp.sum(found_ref[...].astype(F32), axis=0)
     scaled = (x * gain_ref[...].astype(F32).reshape(1, columns)).astype(BF16)
     query_ref[...] = jnp.dot(scaled, wq_ref[...], preferred_element_type=F32)
     pair = jnp.dot(scaled, wkv_ref[...], preferred_element_type=F32)
@@ -249,7 +248,6 @@
     vocab, columns = embed_table.shape
     count, width = teacher_rows.shape
     rows_here = groups * count // targets
-    padded = -(-columns // HD) * HD
     half_pad = -(-w_qwen.shape[2] // HD) * HD
     shape = jax.ShapeDtypeStruct
     lines_held = width // HD * count + per
@@ -279,7 +277,7 @@
         [first],
         [near(held), near(table)],
         [pl.BlockSpec((groups, per, HD), lambda i, s: (0, block, 0)), whole_spec(table)],
-        [shape((groups, per, padded), BF16)],
+        [shape((groups, per, columns), BF16)],
     )
     found, w_qwen = lax.optimization_barrier((found, w_qwen))
     found = lax.all_to_all(found, "dp", 0, 0, tiled=True)

time: 88 us -> 88 us (level)
  no operation moved by 1% of the time
where the time goes in v5:
time: 88 us; the launch traced here: 87.6 us
  blocking collectives  54.4 us (62%)
  starting transfers between devices  12.3 us (14%)
  waiting for transfers between devices  9.23 us (10%)
  Pallas kernels  7.32 us (8%)
  local copies, waits for them, and re-layouts  3.41 us (4%)
    all_to_all x1, blocking collectives, shards(): held = lax.all_to_all(held, 'dp', 0, 0, tiled=True)  31.1 us
    all_to_all x1, blocking collectives, shards(): lax.all_to_all(joined, 'tensor', 0, 0, axis_index_groups=lines, tiled=True)  23.3 us
    all_to_all x1, waiting for transfers between devices, shards(): found = lax.all_to_all(found, 'dp', 0, 0, tiled=True)  8.09 us
    pallas_call x5, Pallas kernels, call(): pl.pallas_call(kernel, grid_spec=pltpu.PrefetchScalarGridSpec(num_scalar_...  6.83 us
    all_to_all x1, starting transfers between devices, shards(): found = lax.all_to_all(found, 'dp', 0, 0, tiled=True)  4.54 us
    ppermute x1, starting transfers between devices, shards(): theirs = lax.ppermute(theirs, 'tensor', pairs)  4.3 us
    ppermute x1, starting transfers between devices, shards(): swapped = lax.ppermute(swapped, 'tensor', pairs)  3.47 us
    unnamed x18, local copies, waits for them, and re-layouts  3.26 us
  transfers between devices with their start and end apart: 3, of which 2 were waited for; matrix products, arithmetic and copies ran while one was open for 0% of the time, Pallas kernels for 2%

profile of v5, /device:TPU:1, one launch (start us, length us, event | category | flops | bytes accessed | tf_op | source)
XLA Modules:
  0.0 87.6 jit_solution(2237020120486254204)
XLA Ops:
  0.6 0.0 copy-start.1
  0.6 0.1 pad_add_fusion.place_ref
  0.7 1.0 %shard_map.148 = bf16[32,72,128]{2,1,0:T(8,128)(2,1)S(1)} custom-call(s32[2,4]{1,0:T(2,128)} %tokens_ref.1, s32[1,4]{1,0:T(1,128)} %lens_ref.1, s32[1,4]{1,0:T(1,128)} %kinds_ref.1, bf16[16,512]{1,0:T(8,128)(2,1)} %rows_ref.1), custom_call_target="tpu_custom_call" | custom-call | tf_op jit(solution)/shard_map/pallas_call | solution.py:214
  1.7 31.1 %all_to_all.15.info_ref = bf16[32,72,128]{2,1,0:T(8,128)(2,1)S(1)} all-to-all(bf16[32,72,128]{2,1,0:T(8,128)(2,1)S(1)} %shard_map.148), channel_id=1, replica_groups=mesh['dp'=32,'tensor'=16] {'dp'}, dimensions={0} | all-to-all | bytes 1179648 | tf_op jit(solution)/shard_map/all_to_all | solution.py:269
  32.8 0.0 copy-start.8
  32.8 0.0 copy-done.1
  32.8 1.3 %shard_map.149 = bf16[32,8,224]{2,1,0:T(8,128)(2,1)} custom-call(s32[1]{0:T(128)} %bitcast.first_ref, bf16[32,72,128]{2,1,0:T(8,128)(2,1)S(1)} %all_to_all.15.info_ref, bf16[224,2432]{1,0:T(8,128)(2,1)S(1)} %bitcast.18), custom_call_target="tpu_custom_call" | custom-call | tf_op jit(solution)/shard_map/pallas_call | solution.py:214
  34.1 0.0 copy-done.8
  34.1 0.0 copy-start
  34.1 0.1 copy.18
  34.3 1.0 %copy-done = bf16[512,2,448]{0,2,1:T(8,128)(2,1)S(1)} copy-done((bf16[512,2,448]{0,2,1:T(8,128)(2,1)S(1)}, bf16[512,2,448]{0,2,1:T(8,128)(2,1)}, u32[]{:S(2)}) %copy-start) | copy-done | bytes 917528
  35.3 0.7 shard_map.150
  36.0 4.3 %collective-permute-start = (bf16[8,32,1024]{2,1,0:T(8,128)(2,1)S(1)}, bf16[8,32,1024]{2,1,0:T(8,128)(2,1)}, u32[]{:S(2)}, u32[]{:S(2)}) collective-permute-start(bf16[8,32,1024]{2,1,0:T(8,128)(2,1)S(1)} %shard_map.150), channel_id=1, source_target_pairs={{0,1},{1,0},{2,3},{3,2},{4,5},{5,4},{6,7},{7,6},{8,9},{9,8},{10,11... | collective-permute-start | bytes 1572872 | tf_op jit(solution)/shard_map/ppermute | solution.py:298
  40.3 4.5 %all-to-all-start.1 = ((bf16[32,8,224]{2,1,0:T(8,128)(2,1)}), bf16[32,8,224]{2,1,0:T(8,128)(2,1)S(1)}, u32[]{:S(2)}, u32[]{:S(2)}) async-start(bf16[32,8,224]{2,1,0:T(8,128)(2,1)} %shard_map.149), calls=%async_computation.1 | async-start | bytes 262144 | tf_op jit(solution)/shard_map/all_to_all | solution.py:283
  44.9 0.0 copy-start.6
  44.9 0.0 collective-permute-done.rest_0_
  44.9 1.8 %shard_map.151 = bf16[8,32,1024]{2,1,0:T(8,128)(2,1)S(1)} custom-call(s32[1]{0:T(128)} %bitcast.1.side_ref, bf16[8,2,2,72,128]{4,3,2,1,0:T(8,128)(2,1)S(1)} %bitcast.12, bf16[2,448,512]{2,1,0:T(8,128)(2,1)S(1)} %bitcast.17, bf16[2,462,512]{2,1,0:T(8,128)(2,1)S(1)} %bitcast.15, bf16[8,32,1024]{2,1,0:T(8,128)(2,1)} %collective-permute-done.rest_0_), custom_call_target="tpu_custom_call" | custom-call | tf_op jit(solution)/shard_map/pallas_call | solution.py:214
  46.7 8.1 %all-to-all-done.1.found_ref = bf16[32,8,224]{2,1,0:T(8,128)(2,1)S(1)} async-done(((bf16[32,8,224]{2,1,0:T(8,128)(2,1)}), bf16[32,8,224]{2,1,0:T(8,128)(2,1)S(1)}, u32[]{:S(2)}, u32[]{:S(2)}) %all-to-all-start.1) | async-done | bytes 114720 | tf_op jit(solution)/shard_map/all_to_all | solution.py:283
  54.8 0.0 copy-done.6
  54.8 0.0 copy-start.2
  54.8 1.2 %copy-done.2 = bf16[224,2048]{1,0:T(8,128)(2,1)S(1)} copy-done((bf16[224,2048]{1,0:T(8,128)(2,1)S(1)}, bf16[224,2048]{1,0:T(8,128)(2,1)}, u32[]{:S(2)}) %copy-start.2) | copy-done | bytes 917528
  56.0 0.0 copy-start.3
  56.0 1.0 %copy-done.3 = bf16[224,1024]{1,0:T(8,128)(2,1)S(1)} copy-done((bf16[224,1024]{1,0:T(8,128)(2,1)S(1)}, bf16[224,1024]{1,0:T(8,128)(2,1)}, u32[]{:S(2)}) %copy-start.3) | copy-done | bytes 458776
  57.0 0.5 student.1
  57.5 0.0 copy-start.4
  57.5 0.0 copy-start.5
  57.5 0.0 copy-start.7
  57.5 3.5 %collective-permute-start.1 = (f32[8,32,256]{2,1,0:T(8,128)S(1)}, f32[8,32,256]{2,1,0:T(8,128)S(1)}, u32[]{:S(2)}, u32[]{:S(2)}) collective-permute-start(f32[8,32,256]{2,1,0:T(8,128)S(1)} %get-tuple-element.38), channel_id=1, source_target_pairs={{0,1},{1,0},{2,3},{3,2},{4,5},{5,4},{6,7},{7,6},{8,9},{9,8},{10,11... | collective-permute-start | bytes 786440 | tf_op jit(solution)/shard_map/ppermute | solution.py:320
  61.0 1.1 %collective-permute-done.1 = f32[8,32,256]{2,1,0:T(8,128)S(1)} collective-permute-done((f32[8,32,256]{2,1,0:T(8,128)S(1)}, f32[8,32,256]{2,1,0:T(8,128)S(1)}, u32[]{:S(2)}, u32[]{:S(2)}) %collective-permute-start.1) | collective-permute-done | bytes 262176 | tf_op jit(solution)/shard_map/ppermute | solution.py:320
  62.2 23.3 %all_to_all.16.parts_ref = bf16[8,32,1024]{2,1,0:T(8,128)(2,1)S(1)} all-to-all(bf16[8,32,1024]{2,1,0:T(8,128)(2,1)S(1)} %fusion), channel_id=1, replica_groups={{0,2,4,6,8,10,12,14},{1,3,5,7,9,11,13,15},{16,18,20,22,24,26,28,30},{17..., dimensions={0} | all-to-all | bytes 1048576 | tf_op jit(solution)/shard_map/all_to_all | solution.py:327
  85.6 0.0 copy-done.4
  85.6 0.0 copy-done.5
  85.6 0.0 copy-done.7
  85.6 2.0 %shard_map.152 = (bf16[2,4,128]{2,1,0:T(4,128)(2,1)}, bf16[32,448]{1,0:T(8,128)(2,1)}, bf16[32,462]{1,0:T(8,128)(2,1)}) custom-call(s32[2]{0:T(128)S(1)} %pad_add_fusion.place_ref, s32[2]{0:T(128)S(1)} %copy-done.7, bf16[8,32,1024]{2,1,0:T(8,128)(2,1)S(1)} %all_to_all.16.parts_ref, bf16[16,2,72,128]{3,2,1,0:T(8,128)(2,1)S(1)} %bitcast.13, ...), custom_call_target="tpu_custom_call" | custom-call | tf_op jit(solution)/shard_map/pallas_call | solution.py:214
  (1 shorter events, 0.0 us)
Async XLA Ops:
  0.6 32.2 %copy-start.1 = (bf16[2432,224]{0,1:T(8,128)(2,1)S(1)}, bf16[2432,224]{0,1:T(8,128)(2,1)}, u32[]{:S(2)}) copy-start(bf16[2432,224]{0,1:T(8,128)(2,1)} %param.14) | copy-start | bytes 3268612
  32.8 1.3 %copy-start.8 = (bf16[512,2,462]{0,1,2:T(2,128)(2,1)S(1)}, bf16[512,2,462]{0,1,2:T(2,128)(2,1)}, u32[]{:S(2)}) copy-start(bf16[512,2,462]{0,1,2:T(2,128)(2,1)} %param.23) | copy-start | bytes 2838532
  34.1 1.2 %copy-start = (bf16[512,2,448]{0,2,1:T(8,128)(2,1)S(1)}, bf16[512,2,448]{0,2,1:T(8,128)(2,1)}, u32[]{:S(2)}) copy-start(bf16[512,2,448]{0,2,1:T(8,128)(2,1)} %param.22) | copy-start | bytes 2752516
  36.0 8.9 %collective-permute-start = (bf16[8,32,1024]{2,1,0:T(8,128)(2,1)S(1)}, bf16[8,32,1024]{2,1,0:T(8,128)(2,1)}, u32[]{:S(2)}, u32[]{:S(2)}) collective-permute-start(bf16[8,32,1024]{2,1,0:T(8,128)(2,1)S(1)} %shard_map.150), channel_id=1, source_target_pairs={{0,1},{1,0},{2,3},{3,2},{4,5},{5,4},{6,7},{7,6},{8,9},{9,8},{10,11... | collective-permute-start | bytes 1572872 | tf_op jit(solution)/shard_map/ppermute | solution.py:298
  40.3 14.5 %all-to-all-start.1 = ((bf16[32,8,224]{2,1,0:T(8,128)(2,1)}), bf16[32,8,224]{2,1,0:T(8,128)(2,1)S(1)}, u32[]{:S(2)}, u32[]{:S(2)}) async-start(bf16[32,8,224]{2,1,0:T(8,128)(2,1)} %shard_map.149), calls=%async_computation.1 | async-start | bytes 262144 | tf_op jit(solution)/shard_map/all_to_all | solution.py:283
  44.9 9.9 %copy-start.6 = (bf16[224]{0:T(256)(128)(2,1)S(1)}, bf16[224]{0:T(256)(128)(2,1)}, u32[]{:S(2)}) copy-start(bf16[224]{0:T(256)(128)(2,1)} %gain_ref) | copy-start | bytes 1348
  54.8 1.2 %copy-start.2 = (bf16[224,2048]{1,0:T(8,128)(2,1)S(1)}, bf16[224,2048]{1,0:T(8,128)(2,1)}, u32[]{:S(2)}) copy-start(bf16[224,2048]{1,0:T(8,128)(2,1)} %wq_ref.1) | copy-start | bytes 2752516
  56.0 1.0 %copy-start.3 = (bf16[224,1024]{1,0:T(8,128)(2,1)S(1)}, bf16[224,1024]{1,0:T(8,128)(2,1)}, u32[]{:S(2)}) copy-start(bf16[224,1024]{1,0:T(8,128)(2,1)} %wkv_ref.1) | copy-start | bytes 1376260
  57.5 28.1 %copy-start.4 = (bf16[2,4,64,128]{3,2,1,0:T(8,128)(2,1)S(1)}, bf16[2,4,64,128]{3,2,1,0:T(8,128)(2,1)}, u32[]{:S(2)}) copy-start(bf16[2,4,64,128]{3,2,1,0:T(8,128)(2,1)} %keys_ref.1) | copy-start | bytes 393220
  57.5 28.0 %copy-start.5 = (bf16[2,4,64,128]{3,2,1,0:T(8,128)(2,1)S(1)}, bf16[2,4,64,128]{3,2,1,0:T(8,128)(2,1)}, u32[]{:S(2)}) copy-start(bf16[2,4,64,128]{3,2,1,0:T(8,128)(2,1)} %values_ref.1) | copy-start | bytes 393220
  57.5 28.0 %copy-start.7 = (s32[2]{0:T(128)S(1)}, s32[2]{0:T(128)}, u32[]{:S(2)}) copy-start(s32[2]{0:T(128)} %sizes_ref) | copy-start | bytes 28
  57.5 4.6 %collective-permute-start.1 = (f32[8,32,256]{2,1,0:T(8,128)S(1)}, f32[8,32,256]{2,1,0:T(8,128)S(1)}, u32[]{:S(2)}, u32[]{:S(2)}) collective-permute-start(f32[8,32,256]{2,1,0:T(8,128)S(1)} %get-tuple-element.38), channel_id=1, source_target_pairs={{0,1},{1,0},{2,3},{3,2},{4,5},{5,4},{6,7},{7,6},{8,9},{9,8},{10,11... | collective-permute-start | bytes 786440 | tf_op jit(solution)/shard_map/ppermute | solution.py:320

commit v6 on v5

--- a/solution.py
+++ b/solution.py
@@ -178,23 +178,29 @@
     col = lax.broadcasted_iota(jnp.int32, (per, per), 1)
     fits = jnp.logical_and(row // steps == col // steps, col <= row)
     score_new = jnp.where(fits, score_new, -jnp.inf)
+    keys = keys_ref[:, 0].reshape(rollouts * slots, HD)
+    values = values_ref[:, 0].reshape(rollouts * slots, HD)
+    score = nt_dot(query, keys) * scale
+    row = lax.broadcasted_iota(jnp.int32, score.shape, 0)
+    slot = lax.broadcasted_iota(jnp.int32, score.shape, 1)
+    live = jnp.zeros(score.shape, jnp.bool_)
     for b in range(rollouts):
-        score = nt_dot(query, keys_ref[b, 0]) * scale
-        slot = lax.broadcasted_iota(jnp.int32, (per, slots), 1)
-        score = jnp.where(slot < sizes_ref[b], score, -jnp.inf)
-        mine = score_new[b * steps : (b + 1) * steps]
-        score = score[b * steps : (b + 1) * steps]
-        top = jnp.maximum(
-            jnp.max(score, axis=1, keepdims=True), jnp.max(mine, axis=1, keepdims=True)
-        )
-        old_exp = jnp.exp(score - top)
-        new_exp = jnp.exp(mine - top)
-        whole = jnp.sum(old_exp, axis=1, keepdims=True) + jnp.sum(new_exp, axis=1, keepdims=True)
-        old = (old_exp / whole).astype(BF16)
-        new = (new_exp / whole).astype(BF16)
-        mixed = jnp.dot(old, values_ref[b, 0], preferred_element_type=F32)
-        mixed = mixed + jnp.dot(new, value, preferred_element_type=F32)
-        attn_ref[b] = mixed.astype(BF16)
+        mine = jnp.logical_and(row >= b * steps, row < (b + 1) * steps)
+        held = jnp.logical_and(slot >= b * slots, slot < b * slots + sizes_ref[b])
+        live = jnp.logical_or(live, jnp.logical_and(mine, held))
+    score = jnp.where(live, score, -jnp.inf)
+    top = jnp.maximum(
+        jnp.max(score, axis=1, keepdims=True), jnp.max(score_new, axis=1, keepdims=True)
+    )
+    old_exp = jnp.exp(score - top)
+    new_exp = jnp.exp(score_new - top)
+    whole = jnp.sum(old_exp, axis=1, keepdims=True) + jnp.sum(new_exp, axis=1, keepdims=True)
+    old = (old_exp / whole).astype(BF16)
+    new = (new_exp / whole).astype(BF16)
+    mixed = jnp.dot(old, values, preferred_element_type=F32)
+    mixed = mixed + jnp.dot(new, value, preferred_element_type=F32)
+    for b in range(rollouts):
+        attn_ref[b] = mixed[b * steps : (b + 1) * steps].astype(BF16)
 
 
 def near(array):

time: 88 us -> 87.7 us (level)
  no operation moved by 1% of the time
where the time goes in v6:
time: 87.7 us; the launch traced here: 87.3 us
  blocking collectives  54.4 us (62%)
  starting transfers between devices  12.3 us (14%)
  waiting for transfers between devices  9.23 us (11%)
  Pallas kernels  7.03 us (8%)
  local copies, waits for them, and re-layouts  3.41 us (4%)
    all_to_all x1, blocking collectives, shards(): held = lax.all_to_all(held, 'dp', 0, 0, tiled=True)  31.1 us
    all_to_all x1, blocking collectives, shards(): lax.all_to_all(joined, 'tensor', 0, 0, axis_index_groups=lines, tiled=True)  23.3 us
    all_to_all x1, waiting for transfers between devices, shards(): found = lax.all_to_all(found, 'dp', 0, 0, tiled=True)  8.09 us
    pallas_call x5, Pallas kernels, call(): pl.pallas_call(kernel, grid_spec=pltpu.PrefetchScalarGridSpec(num_scalar_...  6.53 us
    all_to_all x1, starting transfers between devices, shards(): found = lax.all_to_all(found, 'dp', 0, 0, tiled=True)  4.54 us
    ppermute x1, starting transfers between devices, shards(): theirs = lax.ppermute(theirs, 'tensor', pairs)  4.3 us
    ppermute x1, starting transfers between devices, shards(): swapped = lax.ppermute(swapped, 'tensor', pairs)  3.47 us
    unnamed x18, local copies, waits for them, and re-layouts  3.26 us
  transfers between devices with their start and end apart: 3, of which 2 were waited for; matrix products, arithmetic and copies ran while one was open for 0% of the time, Pallas kernels for 2%

profile of v6, /device:TPU:1, one launch (start us, length us, event | category | flops | bytes accessed | tf_op | source)
XLA Modules:
  0.0 87.3 jit_solution(16827130666277049835)
XLA Ops:
  0.6 0.0 copy-start.1
  0.6 0.1 pad_add_fusion.place_ref
  0.7 1.0 %shard_map.148 = bf16[32,72,128]{2,1,0:T(8,128)(2,1)S(1)} custom-call(s32[2,4]{1,0:T(2,128)} %tokens_ref.1, s32[1,4]{1,0:T(1,128)} %lens_ref.1, s32[1,4]{1,0:T(1,128)} %kinds_ref.1, bf16[16,512]{1,0:T(8,128)(2,1)} %rows_ref.1), custom_call_target="tpu_custom_call" | custom-call | tf_op jit(solution)/shard_map/pallas_call | solution.py:220
  1.7 31.1 %all_to_all.15.info_ref = bf16[32,72,128]{2,1,0:T(8,128)(2,1)S(1)} all-to-all(bf16[32,72,128]{2,1,0:T(8,128)(2,1)S(1)} %shard_map.148), channel_id=1, replica_groups=mesh['dp'=32,'tensor'=16] {'dp'}, dimensions={0} | all-to-all | bytes 1179648 | tf_op jit(solution)/shard_map/all_to_all | solution.py:275
  32.8 0.0 copy-start.8
  32.8 0.0 copy-done.1
  32.8 1.3 %shard_map.149 = bf16[32,8,224]{2,1,0:T(8,128)(2,1)} custom-call(s32[1]{0:T(128)} %bitcast.first_ref, bf16[32,72,128]{2,1,0:T(8,128)(2,1)S(1)} %all_to_all.15.info_ref, bf16[224,2432]{1,0:T(8,128)(2,1)S(1)} %bitcast.18), custom_call_target="tpu_custom_call" | custom-call | tf_op jit(solution)/shard_map/pallas_call | solution.py:220
  34.1 0.0 copy-done.8
  34.1 0.0 copy-start
  34.1 0.1 copy.18
  34.3 1.0 %copy-done = bf16[512,2,448]{0,2,1:T(8,128)(2,1)S(1)} copy-done((bf16[512,2,448]{0,2,1:T(8,128)(2,1)S(1)}, bf16[512,2,448]{0,2,1:T(8,128)(2,1)}, u32[]{:S(2)}) %copy-start) | copy-done | bytes 917528
  35.3 0.7 shard_map.150
  36.0 4.3 %collective-permute-start = (bf16[8,32,1024]{2,1,0:T(8,128)(2,1)S(1)}, bf16[8,32,1024]{2,1,0:T(8,128)(2,1)}, u32[]{:S(2)}, u32[]{:S(2)}) collective-permute-start(bf16[8,32,1024]{2,1,0:T(8,128)(2,1)S(1)} %shard_map.150), channel_id=1, source_target_pairs={{0,1},{1,0},{2,3},{3,2},{4,5},{5,4},{6,7},{7,6},{8,9},{9,8},{10,11... | collective-permute-start | bytes 1572872 | tf_op jit(solution)/shard_map/ppermute | solution.py:304
  40.3 4.5 %all-to-all-start.1 = ((bf16[32,8,224]{2,1,0:T(8,128)(2,1)}), bf16[32,8,224]{2,1,0:T(8,128)(2,1)S(1)}, u32[]{:S(2)}, u32[]{:S(2)}) async-start(bf16[32,8,224]{2,1,0:T(8,128)(2,1)} %shard_map.149), calls=%async_computation.1 | async-start | bytes 262144 | tf_op jit(solution)/shard_map/all_to_all | solution.py:289
  44.9 0.0 copy-start.6
  44.9 0.0 collective-permute-done.rest_0_
  44.9 1.8 %shard_map.151 = bf16[8,32,1024]{2,1,0:T(8,128)(2,1)S(1)} custom-call(s32[1]{0:T(128)} %bitcast.1.side_ref, bf16[8,2,2,72,128]{4,3,2,1,0:T(8,128)(2,1)S(1)} %bitcast.12, bf16[2,448,512]{2,1,0:T(8,128)(2,1)S(1)} %bitcast.17, bf16[2,462,512]{2,1,0:T(8,128)(2,1)S(1)} %bitcast.15, bf16[8,32,1024]{2,1,0:T(8,128)(2,1)} %collective-permute-done.rest_0_), custom_call_target="tpu_custom_call" | custom-call | tf_op jit(solution)/shard_map/pallas_call | solution.py:220
  46.7 8.1 %all-to-all-done.1.found_ref = bf16[32,8,224]{2,1,0:T(8,128)(2,1)S(1)} async-done(((bf16[32,8,224]{2,1,0:T(8,128)(2,1)}), bf16[32,8,224]{2,1,0:T(8,128)(2,1)S(1)}, u32[]{:S(2)}, u32[]{:S(2)}) %all-to-all-start.1) | async-done | bytes 114720 | tf_op jit(solution)/shard_map/all_to_all | solution.py:289
  54.8 0.0 copy-done.6
  54.8 0.0 copy-start.2
  54.8 1.2 %copy-done.2 = bf16[224,2048]{1,0:T(8,128)(2,1)S(1)} copy-done((bf16[224,2048]{1,0:T(8,128)(2,1)S(1)}, bf16[224,2048]{1,0:T(8,128)(2,1)}, u32[]{:S(2)}) %copy-start.2) | copy-done | bytes 917528
  56.0 0.0 copy-start.3
  56.0 1.0 %copy-done.3 = bf16[224,1024]{1,0:T(8,128)(2,1)S(1)} copy-done((bf16[224,1024]{1,0:T(8,128)(2,1)S(1)}, bf16[224,1024]{1,0:T(8,128)(2,1)}, u32[]{:S(2)}) %copy-start.3) | copy-done | bytes 458776
  57.0 0.5 student.1
  57.5 0.0 copy-start.4
  57.5 0.0 copy-start.5
  57.5 0.0 copy-start.7
  57.5 3.5 %collective-permute-start.1 = (f32[8,32,256]{2,1,0:T(8,128)S(1)}, f32[8,32,256]{2,1,0:T(8,128)S(1)}, u32[]{:S(2)}, u32[]{:S(2)}) collective-permute-start(f32[8,32,256]{2,1,0:T(8,128)S(1)} %get-tuple-element.38), channel_id=1, source_target_pairs={{0,1},{1,0},{2,3},{3,2},{4,5},{5,4},{6,7},{7,6},{8,9},{9,8},{10,11... | collective-permute-start | bytes 786440 | tf_op jit(solution)/shard_map/ppermute | solution.py:326
  61.0 1.1 %collective-permute-done.1 = f32[8,32,256]{2,1,0:T(8,128)S(1)} collective-permute-done((f32[8,32,256]{2,1,0:T(8,128)S(1)}, f32[8,32,256]{2,1,0:T(8,128)S(1)}, u32[]{:S(2)}, u32[]{:S(2)}) %collective-permute-start.1) | collective-permute-done | bytes 262176 | tf_op jit(solution)/shard_map/ppermute | solution.py:326
  62.2 23.3 %all_to_all.16.parts_ref = bf16[8,32,1024]{2,1,0:T(8,128)(2,1)S(1)} all-to-all(bf16[8,32,1024]{2,1,0:T(8,128)(2,1)S(1)} %fusion), channel_id=1, replica_groups={{0,2,4,6,8,10,12,14},{1,3,5,7,9,11,13,15},{16,18,20,22,24,26,28,30},{17..., dimensions={0} | all-to-all | bytes 1048576 | tf_op jit(solution)/shard_map/all_to_all | solution.py:333
  85.6 0.0 copy-done.4
  85.6 0.0 copy-done.5
  85.6 0.0 copy-done.7
  85.6 1.7 %shard_map.152 = (bf16[2,4,128]{2,1,0:T(4,128)(2,1)}, bf16[32,448]{1,0:T(8,128)(2,1)}, bf16[32,462]{1,0:T(8,128)(2,1)}) custom-call(s32[2]{0:T(128)S(1)} %pad_add_fusion.place_ref, s32[2]{0:T(128)S(1)} %copy-done.7, bf16[8,32,1024]{2,1,0:T(8,128)(2,1)S(1)} %all_to_all.16.parts_ref, bf16[16,2,72,128]{3,2,1,0:T(8,128)(2,1)S(1)} %bitcast.13, ...), custom_call_target="tpu_custom_call" | custom-call | tf_op jit(solution)/shard_map/pallas_call | solution.py:220
  (1 shorter events, 0.0 us)
Async XLA Ops:
  0.6 32.2 %copy-start.1 = (bf16[2432,224]{0,1:T(8,128)(2,1)S(1)}, bf16[2432,224]{0,1:T(8,128)(2,1)}, u32[]{:S(2)}) copy-start(bf16[2432,224]{0,1:T(8,128)(2,1)} %param.14) | copy-start | bytes 3268612
  32.8 1.3 %copy-start.8 = (bf16[512,2,462]{0,1,2:T(2,128)(2,1)S(1)}, bf16[512,2,462]{0,1,2:T(2,128)(2,1)}, u32[]{:S(2)}) copy-start(bf16[512,2,462]{0,1,2:T(2,128)(2,1)} %param.23) | copy-start | bytes 2838532
  34.1 1.2 %copy-start = (bf16[512,2,448]{0,2,1:T(8,128)(2,1)S(1)}, bf16[512,2,448]{0,2,1:T(8,128)(2,1)}, u32[]{:S(2)}) copy-start(bf16[512,2,448]{0,2,1:T(8,128)(2,1)} %param.22) | copy-start | bytes 2752516
  36.0 8.9 %collective-permute-start = (bf16[8,32,1024]{2,1,0:T(8,128)(2,1)S(1)}, bf16[8,32,1024]{2,1,0:T(8,128)(2,1)}, u32[]{:S(2)}, u32[]{:S(2)}) collective-permute-start(bf16[8,32,1024]{2,1,0:T(8,128)(2,1)S(1)} %shard_map.150), channel_id=1, source_target_pairs={{0,1},{1,0},{2,3},{3,2},{4,5},{5,4},{6,7},{7,6},{8,9},{9,8},{10,11... | collective-permute-start | bytes 1572872 | tf_op jit(solution)/shard_map/ppermute | solution.py:304
  40.3 14.5 %all-to-all-start.1 = ((bf16[32,8,224]{2,1,0:T(8,128)(2,1)}), bf16[32,8,224]{2,1,0:T(8,128)(2,1)S(1)}, u32[]{:S(2)}, u32[]{:S(2)}) async-start(bf16[32,8,224]{2,1,0:T(8,128)(2,1)} %shard_map.149), calls=%async_computation.1 | async-start | bytes 262144 | tf_op jit(solution)/shard_map/all_to_all | solution.py:289
  44.9 9.9 %copy-start.6 = (bf16[224]{0:T(256)(128)(2,1)S(1)}, bf16[224]{0:T(256)(128)(2,1)}, u32[]{:S(2)}) copy-start(bf16[224]{0:T(256)(128)(2,1)} %gain_ref) | copy-start | bytes 1348
  54.8 1.2 %copy-start.2 = (bf16[224,2048]{1,0:T(8,128)(2,1)S(1)}, bf16[224,2048]{1,0:T(8,128)(2,1)}, u32[]{:S(2)}) copy-start(bf16[224,2048]{1,0:T(8,128)(2,1)} %wq_ref.1) | copy-start | bytes 2752516
  56.0 1.0 %copy-start.3 = (bf16[224,1024]{1,0:T(8,128)(2,1)S(1)}, bf16[224,1024]{1,0:T(8,128)(2,1)}, u32[]{:S(2)}) copy-start(bf16[224,1024]{1,0:T(8,128)(2,1)} %wkv_ref.1) | copy-start | bytes 1376260
  57.5 28.1 %copy-start.4 = (bf16[2,4,64,128]{3,2,1,0:T(8,128)(2,1)S(1)}, bf16[2,4,64,128]{3,2,1,0:T(8,128)(2,1)}, u32[]{:S(2)}) copy-start(bf16[2,4,64,128]{3,2,1,0:T(8,128)(2,1)} %keys_ref.1) | copy-start | bytes 393220
  57.5 28.0 %copy-start.5 = (bf16[2,4,64,128]{3,2,1,0:T(8,128)(2,1)S(1)}, bf16[2,4,64,128]{3,2,1,0:T(8,128)(2,1)}, u32[]{:S(2)}) copy-start(bf16[2,4,64,128]{3,2,1,0:T(8,128)(2,1)} %values_ref.1) | copy-start | bytes 393220
  57.5 28.0 %copy-start.7 = (s32[2]{0:T(128)S(1)}, s32[2]{0:T(128)}, u32[]{:S(2)}) copy-start(s32[2]{0:T(128)} %sizes_ref) | copy-start | bytes 28
  57.5 4.6 %collective-permute-start.1 = (f32[8,32,256]{2,1,0:T(8,128)S(1)}, f32[8,32,256]{2,1,0:T(8,128)S(1)}, u32[]{:S(2)}, u32[]{:S(2)}) collective-permute-start(f32[8,32,256]{2,1,0:T(8,128)S(1)} %get-tuple-element.38), channel_id=1, source_target_pairs={{0,1},{1,0},{2,3},{3,2},{4,5},{5,4},{6,7},{7,6},{8,9},{9,8},{10,11... | collective-permute-start | bytes 786440 | tf_op jit(solution)/shard_map/ppermute | solution.py:326
